TPU v7x, 512 devices: a whole 4x4x16 slice. The times are simulated.
512 devices in a mesh: gx: 16 (over z), gy: 4 (over x), gz: 8 (over y, core).
Axes of the slice: x: 4, y: 4, z: 16, core: 2. Of those that a mesh axis runs over, the one named last changes fastest.
Arguments:
- flow: float32 [4, 128, 64, 1024], P(None, 'gx', 'gy', 'gz'), may hold values from -3 to 3
- basis: float32 [127, 3, 131072], P(None, None, ('gx', 'gy', 'gz')), may hold values from -1150 to 1150
- sample: int32 [131072], P(('gx', 'gy', 'gz')), may hold values from 0 to 16383
Outputs:
- flow_next: float32 [4, 128, 64, 1024], P(None, 'gx', 'gy', 'gz')
- basis_next: float32 [128, 3, 131072], P(None, None, ('gx', 'gy', 'gz'))
- factor: float32 [128, 128], replicated
All inputs are finite; a program needn't handle non-finite values.
Results may differ from a plain program's by a relative error of at most 0.000065.
Values sent between devices are 32-bit elements; how exact they have to be, the bound alone decides.
A program may use at most 64 MiB of HBM per device.

v0:
```python
import jax
import jax.numpy as jnp
from jax import lax
from jax.sharding import PartitionSpec as P

DT_STEP = 0.35
VISCOSITY = 0.2
SOUND_SQ = 1.0
DRIVING = 0.5


def padded(block, sides, width, periodic):
    for axis, dim in sides:
        count = lax.axis_size(axis)
        forward = [(i, i + 1) for i in range(count - 1)]
        if periodic:
            forward.append((count - 1, 0))
        backward = [(target, source) for source, target in forward]
        low = lax.ppermute(
            lax.slice_in_dim(block, block.shape[dim] - width, None, axis=dim), axis, forward
        )
        high = lax.ppermute(lax.slice_in_dim(block, 0, width, axis=dim), axis, backward)
        block = jnp.concatenate([low, block, high], axis=dim)
    return block


def rates(ext):
    centre = ext[:, 1:-1, 1:-1, 1:-1]
    x_plus = ext[:, 2:, 1:-1, 1:-1]
    x_minus = ext[:, :-2, 1:-1, 1:-1]
    y_plus = ext[:, 1:-1, 2:, 1:-1]
    y_minus = ext[:, 1:-1, :-2, 1:-1]
    z_plus = ext[:, 1:-1, 1:-1, 2:]
    z_minus = ext[:, 1:-1, 1:-1, :-2]
    slope_x = 0.5 * (x_plus - x_minus)
    slope_y = 0.5 * (y_plus - y_minus)
    slope_z = 0.5 * (z_plus - z_minus)
    laplace = x_plus + x_minus + (y_plus + y_minus) + (z_plus + z_minus) - 6.0 * centre
    advect = centre[0] * slope_x[:3] + centre[1] * slope_y[:3] + centre[2] * slope_z[:3]
    pressure = jnp.stack([slope_x[3], slope_y[3], slope_z[3]])
    forcing = jnp.array([DRIVING, 0.0, 0.0], dtype=jnp.float32).reshape(3, 1, 1, 1)
    velocity = VISCOSITY * laplace[:3] - advect - pressure + forcing
    density = -SOUND_SQ * (slope_x[0] + slope_y[1] + slope_z[2])
    return jnp.concatenate([velocity, density[None]], axis=0)


def extend_one(fields):
    walled = padded(fields, (("gy", 2),), 1, False)
    return padded(walled, (("gx", 1), ("gz", 3)), 1, True)


def local(flow, basis, sample):
    points = basis.shape[2]
    modes = basis.shape[0]
    count = 3.0 * points * lax.axis_size("gx") * lax.axis_size("gy") * lax.axis_size("gz")
    section_one = flow + DT_STEP * rates(extend_one(flow))
    section_two = 0.75 * flow + 0.25 * (section_one + DT_STEP * rates(extend_one(section_one)))
    flow_next = 1.0 / 3.0 * flow + 2.0 / 3.0 * (
        section_two + DT_STEP * rates(extend_one(section_two))
    )
    velocity = flow_next[:3].reshape(3, -1)
    snapshot = jnp.take(velocity, sample, axis=1)
    stacked = jnp.concatenate([basis, snapshot[None]], axis=0).reshape(modes + 1, 3 * points)
    local_gram = jnp.dot(
        stacked, stacked.T, precision=lax.Precision.HIGHEST, preferred_element_type=jnp.float32
    )
    gram = lax.psum(local_gram, ("gx", "gy", "gz")) / count
    lower = jnp.linalg.cholesky(gram)
    basis_next = jax.scipy.linalg.solve_triangular(lower, stacked, lower=True).reshape(
        modes + 1, 3, points
    )
    return (flow_next, basis_next, lower.T)


def solution(mesh):
    return jax.shard_map(
        local,
        mesh=mesh,
        in_specs=(
            P(None, "gx", "gy", "gz"),
            P(None, None, ("gx", "gy", "gz")),
            P(("gx", "gy", "gz")),
        ),
        out_specs=(P(None, "gx", "gy", "gz"), P(None, None, ("gx", "gy", "gz")), P()),
        check_vma=False,
    )
```

profile of v0, /device:TPU:1, one launch (start us, length us, event | category | flops | bytes accessed | tf_op | source)
XLA Modules:
  0.0 582.4 jit_solution(7620865436270588193)
XLA Ops:
  8.3 3.9 collective-permute-start
  12.2 1.3 collective-permute-start.1
  14.4 2.2 collective-permute-done.1
  17.5 11.1 %collective-permute-start.2 = (f32[4,1,18,128]{3,2,1,0:T(8,128)S(1)}, f32[4,1,18,128]{3,2,1,0:T(8,128)S(1)}, u32[]{:S(2)}, u32[]{:S(2)}) collective-permute-start(f32[4,1,18,128]{3,2,1,0:T(8,128)S(1)} %get-tuple-element.41), channel_id=1, source_target_pairs={{32,0},{64,32},{96,64},{128,96},{160,128},{192,160},{224,192},{256... | collective-permute-start | bytes 110600 | tf_op jit(solution)/shard_map/ppermute | solution.py:22
  28.6 1.9 collective-permute-start.3
  31.2 3.4 collective-permute-done.3
  35.9 3.5 collective-permute-start.4
  40.6 1.6 subtract_multiply_fusion.5
  42.2 5.2 collective-permute-done.4
  47.4 1.4 subtract_multiply_fusion.4
  48.9 1.5 fusion.24
  50.4 3.1 collective-permute-start.6
  53.6 1.3 collective-permute-start.7
  54.9 3.1 collective-permute-done.7
  58.1 1.9 collective-permute-start.8
  60.0 3.4 collective-permute-start.9
  63.4 2.6 collective-permute-done.9
  66.3 4.2 collective-permute-start.10
  70.7 6.5 %collective-permute-done.10 = f32[4,10,18,1]{3,2,1,0:T(8,128)S(1)} collective-permute-done((f32[4,10,18,1]{3,2,1,0:T(8,128)S(1)}, f32[4,10,18,1]{3,2,1,0:T(8,128)S(1)}, u32[]{:S(2)}, u32[]{:S(2)}) %collective-permute-start.10) | collective-permute-done | bytes 2912 | tf_op jit(solution)/shard_map/ppermute | solution.py:22
  77.9 2.8 collective-permute-start.12
  80.7 1.3 collective-permute-start.13
  82.2 3.0 collective-permute-done.13
  85.2 1.9 collective-permute-start.14
  87.1 3.5 collective-permute-start.15
  90.7 2.5 collective-permute-done.15
  93.4 5.4 collective-permute-start.16
  99.0 5.4 collective-permute-done.16
  105.3 4.7 copy.16
  110.1 4.1 gather_fusion
  115.8 433.1 %all-reduce.2.cloned.1.call-done = f32[128,128]{0,1:T(8,128)} async-done(((f32[128,128]{0,1:T(8,128)}), f32[128,128]{0,1:T(8,128)}) %all-reduce.2.cloned.1.call-update) | async-done | bytes 65552 | tf_op jit(solution)/shard_map/psum | solution.py:67
  550.7 11.7 %cholesky.16 = f32[128,128]{1,0:T(8,128)S(1)} custom-call(f32[128,128]{1,0:T(8,128)S(1)} %fusion.57), custom_call_target="Cholesky" | custom-call | tf_op jit(solution)/shard_map/jit(cholesky)/cholesky | solution.py:68
  563.7 9.8 %custom-call.7 = f32[1,128,128]{1,2,0:T(8,128)S(1)} custom-call(f32[1,128,128]{2,1,0:T(8,128)S(1)} %get-tuple-element.70), custom_call_target="InvertDiagBlocksLowerTriangular" | custom-call | tf_op jit(solution)/shard_map/jit(_solve_triangular)/triangular_solve | solution.py:69
  (71 shorter events, 15.2 us)
Async XLA Ops:
  7.2 43.2 %copy-start = (f32[4,8,16,128]{3,2,1,0:T(8,128)S(1)}, f32[4,8,16,128]{3,2,1,0:T(8,128)}, u32[]{:S(2)}) copy-start(f32[4,8,16,128]{3,2,1,0:T(8,128)} %param.6) | copy-start | bytes 786436
  7.2 47.7 %copy-start.4 = (s32[256]{0:T(256)S(1)}, s32[256]{0:T(256)}, u32[]{:S(2)}) copy-start(s32[256]{0:T(256)} %param.8) | copy-start | bytes 3076
  7.2 541.7 %all-reduce.2.cloned.1.call-start = ((), (), s32[]{:S(2)}) async-start(), calls=%async_computation | async-start | bytes 131072 | tf_op jit(solution)/shard_map/psum | solution.py:67
  8.3 6.2 %collective-permute-start = (f32[4,8,1,128]{3,2,1,0:T(1,128)S(1)}, f32[4,8,1,128]{3,2,1,0:T(1,128)S(1)}, u32[]{:S(2)}, u32[]{:S(2)}) collective-permute-start(f32[4,8,1,128]{3,2,1,0:T(1,128)S(1)} %get-tuple-element.67), channel_id=1, source_target_pairs={{0,8},{8,16},{16,24},{1,9},{9,17},{17,25},{2,10},{10,18},{18,26},{... | collective-permute-start | bytes 49160 | tf_op jit(solution)/shard_map/ppermute | solution.py:19
  12.2 4.5 collective-permute-start.1
  17.5 13.7 %collective-permute-start.2 = (f32[4,1,18,128]{3,2,1,0:T(8,128)S(1)}, f32[4,1,18,128]{3,2,1,0:T(8,128)S(1)}, u32[]{:S(2)}, u32[]{:S(2)}) collective-permute-start(f32[4,1,18,128]{3,2,1,0:T(8,128)S(1)} %get-tuple-element.41), channel_id=1, source_target_pairs={{32,0},{64,32},{96,64},{128,96},{160,128},{192,160},{224,192},{256... | collective-permute-start | bytes 110600 | tf_op jit(solution)/shard_map/ppermute | solution.py:22
  28.6 6.0 %collective-permute-start.3 = (f32[4,1,18,128]{3,2,1,0:T(8,128)S(1)}, f32[4,1,18,128]{3,2,1,0:T(8,128)S(1)}, u32[]{:S(2)}, u32[]{:S(2)}) collective-permute-start(f32[4,1,18,128]{3,2,1,0:T(8,128)S(1)} %get-tuple-element.40), channel_id=1, source_target_pairs={{0,32},{32,64},{64,96},{96,128},{128,160},{160,192},{192,224},{224... | collective-permute-start | bytes 110600 | tf_op jit(solution)/shard_map/ppermute | solution.py:19
  35.7 41.9 %copy-start.3 = (f32[3]{0:T(128)S(1)}, f32[3]{0:T(128)}, u32[]{:S(2)}) copy-start(f32[3]{0:T(128)} %constant.80.clone) | copy-start | bytes 40
  35.9 11.5 %collective-permute-start.4 = (f32[4,10,18,1]{3,2,1,0:T(8,128)S(1)}, f32[4,10,18,1]{3,2,1,0:T(8,128)S(1)}, u32[]{:S(2)}, u32[]{:S(2)}) collective-permute-start(f32[4,10,18,1]{3,2,1,0:T(8,128)S(1)} %get-tuple-element.31), channel_id=1, source_target_pairs={{1,0},{2,1},{3,2},{4,3},{5,4},{6,5},{7,6},{0,7},{9,8},{10,9},{11,1... | collective-permute-start | bytes 8648 | tf_op jit(solution)/shard_map/ppermute | solution.py:22
  39.4 8.0 %collective-permute-start.5 = (f32[4,10,18,1]{3,2,1,0:T(8,128)S(1)}, f32[4,10,18,1]{3,2,1,0:T(8,128)S(1)}, u32[]{:S(2)}, u32[]{:S(2)}) collective-permute-start(f32[4,10,18,1]{3,2,1,0:T(8,128)S(1)} %get-tuple-element.32), channel_id=1, source_target_pairs={{0,1},{1,2},{2,3},{3,4},{4,5},{5,6},{6,7},{7,0},{8,9},{9,10},{10,1... | collective-permute-start | bytes 8648 | tf_op jit(solution)/shard_map/ppermute | solution.py:19
  42.2 39.8 %copy-start.1 = (f32[127,3,256]{2,0,1:T(8,128)S(1)}, f32[127,3,256]{2,0,1:T(8,128)}, u32[]{:S(2)}) copy-start(f32[127,3,256]{2,0,1:T(8,128)} %param.7) | copy-start | bytes 1170436
  50.4 4.5 collective-permute-start.6
  53.6 4.5 collective-permute-start.7
  58.1 5.3 collective-permute-start.8
  60.0 6.0 %collective-permute-start.9 = (f32[4,1,18,128]{3,2,1,0:T(8,128)S(1)}, f32[4,1,18,128]{3,2,1,0:T(8,128)S(1)}, u32[]{:S(2)}, u32[]{:S(2)}) collective-permute-start(f32[4,1,18,128]{3,2,1,0:T(8,128)S(1)} %get-tuple-element.37), channel_id=1, source_target_pairs={{0,32},{32,64},{64,96},{96,128},{128,160},{160,192},{192,224},{224... | collective-permute-start | bytes 110600 | tf_op jit(solution)/shard_map/ppermute | solution.py:19
  66.3 10.9 %collective-permute-start.10 = (f32[4,10,18,1]{3,2,1,0:T(8,128)S(1)}, f32[4,10,18,1]{3,2,1,0:T(8,128)S(1)}, u32[]{:S(2)}, u32[]{:S(2)}) collective-permute-start(f32[4,10,18,1]{3,2,1,0:T(8,128)S(1)} %get-tuple-element.29), channel_id=1, source_target_pairs={{1,0},{2,1},{3,2},{4,3},{5,4},{6,5},{7,6},{0,7},{9,8},{10,9},{11,1... | collective-permute-start | bytes 8648 | tf_op jit(solution)/shard_map/ppermute | solution.py:22
  70.5 6.6 %collective-permute-start.11 = (f32[4,10,18,1]{3,2,1,0:T(8,128)S(1)}, f32[4,10,18,1]{3,2,1,0:T(8,128)S(1)}, u32[]{:S(2)}, u32[]{:S(2)}) collective-permute-start(f32[4,10,18,1]{3,2,1,0:T(8,128)S(1)} %get-tuple-element.30), channel_id=1, source_target_pairs={{0,1},{1,2},{2,3},{3,4},{4,5},{5,6},{6,7},{7,0},{8,9},{9,10},{10,1... | collective-permute-start | bytes 8648 | tf_op jit(solution)/shard_map/ppermute | solution.py:19
  77.9 4.3 collective-permute-start.12
  80.7 4.5 collective-permute-start.13
  85.2 5.5 collective-permute-start.14
  87.1 6.0 %collective-permute-start.15 = (f32[4,1,18,128]{3,2,1,0:T(8,128)S(1)}, f32[4,1,18,128]{3,2,1,0:T(8,128)S(1)}, u32[]{:S(2)}, u32[]{:S(2)}) collective-permute-start(f32[4,1,18,128]{3,2,1,0:T(8,128)S(1)} %get-tuple-element.34), channel_id=1, source_target_pairs={{0,32},{32,64},{64,96},{96,128},{128,160},{160,192},{192,224},{224... | collective-permute-start | bytes 110600 | tf_op jit(solution)/shard_map/ppermute | solution.py:19
  93.4 11.0 %collective-permute-start.16 = (f32[4,10,18,1]{3,2,1,0:T(8,128)S(1)}, f32[4,10,18,1]{3,2,1,0:T(8,128)S(1)}, u32[]{:S(2)}, u32[]{:S(2)}) collective-permute-start(f32[4,10,18,1]{3,2,1,0:T(8,128)S(1)} %get-tuple-element.27), channel_id=1, source_target_pairs={{1,0},{2,1},{3,2},{4,3},{5,4},{6,5},{7,6},{0,7},{9,8},{10,9},{11,1... | collective-permute-start | bytes 8648 | tf_op jit(solution)/shard_map/ppermute | solution.py:22
  98.9 5.8 collective-permute-start.17
  105.3 470.3 %copy-start.2 = (f32[4,8,16,128]{3,2,1,0:T(8,128)}, f32[4,8,16,128]{3,2,1,0:T(8,128)S(1)}, u32[]{:S(2)}) copy-start(f32[4,8,16,128]{3,2,1,0:T(8,128)S(1)} %fusion.15) | copy-start | bytes 786436
Sparse Core Ops, SparseCore 0:
  115.5 433.3 all-reduce.1
where the time goes:
time: 583 us; the launch traced here: 582 us
  waiting for transfers between devices  467 us (80%)
  starting transfers between devices  52 us (9%)
  other arithmetic  33.4 us (6%)
  between operations  14.5 us (2%)
  local copies, waits for them, and re-layouts  12.7 us (2%)
    psum x1, waiting for transfers between devices, local(): gram = lax.psum(local_gram, ('gx', 'gy', 'gz')) / count  433 us
    ppermute x9, starting transfers between devices, padded(): lax.ppermute(lax.slice_in_dim(block, 0, width, axis=dim), axis, backward)  32.1 us
    ppermute x9, waiting for transfers between devices, padded(): lax.ppermute(lax.slice_in_dim(block, 0, width, axis=dim), axis, backward)  25.5 us
    ppermute x9, starting transfers between devices, padded(): lax.ppermute(lax.slice_in_dim(block, block.shape[dim] - width, None, axis...  19.9 us
    another operation x3, other arithmetic, local(): lower = jnp.linalg.cholesky(gram)  12.4 us
  transfers between devices with their start and end apart: 19, of which 11 were waited for; matrix products, arithmetic and copies ran while one was open for 1% of the time, Pallas kernels for 0%

commit v1 on v0

v1 whole, which is shorter than its diff:
```python
import jax
import jax.numpy as jnp
from jax import lax
from jax.experimental import pallas as pl
from jax.experimental.pallas import tpu as pltpu
from jax.sharding import PartitionSpec as P

DT_STEP = 0.35
VISCOSITY = 0.2
SOUND_SQ = 1.0
DRIVING = 0.5
GX, GY, GZ = 16, 4, 8
PLANE = GY * GZ
COUNT = 3.0 * 256 * GX * GY * GZ
MESH = pl.DeviceIdType.MESH
HIGH = lax.Precision.HIGHEST
F32 = jnp.float32


def iota(shape, dim):
    return lax.broadcasted_iota(jnp.int32, shape, dim)


def stencil(field, flow, out, ylo, yhi, zlo, zhi, ynext, gy, weights):
    lane = iota((16, 128), 1)
    lane8 = iota((8, 128), 1)
    row = iota((16, 128), 0)
    low_z, high_z = zlo[...], zhi[...]

    def body(x, faces):
        zl = pltpu.roll(low_z, 64 - 8 * x, 1)
        zh = pltpu.roll(high_z, lax.rem(128 - 8 * x, 128), 1)
        mid = [field[c, x + 1] for c in range(4)]
        sx, sy, sz, lap = [], [], [], []
        for c in range(4):
            a = mid[c]
            xp, xm = field[c, x + 2], field[c, x]
            above = jnp.where(gy < GY - 1, yhi[c, pl.ds(x, 1), :], 0.0)
            below = jnp.where(gy > 0, ylo[c, pl.ds(x, 1), :], 0.0)
            yp = jnp.where(row == 15, above, pltpu.roll(a, 15, 0))
            ym = jnp.where(row == 0, below, pltpu.roll(a, 1, 0))
            m = 2 * c
            left = jnp.concatenate([zl[:, m:m + 1], zl[:, m + 1:m + 2]], axis=0)
            right = jnp.concatenate([zh[:, m:m + 1], zh[:, m + 1:m + 2]], axis=0)
            zp = jnp.where(lane == 127, right, pltpu.roll(a, 127, 1))
            zm = jnp.where(lane == 0, left, pltpu.roll(a, 1, 1))
            sx.append(0.5 * (xp - xm))
            sy.append(0.5 * (yp - ym))
            sz.append(0.5 * (zp - zm))
            if c < 3:
                lap.append(xp + xm + (yp + ym) + (zp + zm) - 6.0 * a)
        press = (sx[3], sy[3], sz[3])
        for c in range(4):
            if c < 3:
                rate = (VISCOSITY * lap[c] - (mid[0] * sx[c] + mid[1] * sy[c] + mid[2] * sz[c])
                        - press[c])
                if c == 0:
                    rate = rate + DRIVING
            else:
                rate = -SOUND_SQ * (sx[0] + sy[1] + sz[2])
            new = mid[c] + DT_STEP * rate
            if weights is not None:
                new = weights[0] * flow[c, x + 1] + weights[1] * new
            if ynext is None:
                out[c, x] = new
            else:
                out[c, x + 1] = new
                faces = pack(new, c, x, faces, lane8, ynext)
        return faces

    return lax.fori_loop(0, 8, body, jnp.zeros((8, 128), F32))


def pack(new, c, x, faces, lane8, ynext):
    ynext[0, c, pl.ds(x, 1), :] = new[0:1]
    ynext[1, c, pl.ds(x, 1), :] = new[15:16]
    for half in range(2):
        tile = new[8 * half:8 * half + 8]
        spot = 8 * x + 2 * c + half
        faces = jnp.where(lane8 == spot, tile[:, 0:1], faces)
        faces = jnp.where(lane8 == spot + 64, tile[:, 127:128], faces)
    return faces


def comm_kernel(flow, bt, sample, out, snap_out, gram_out, row_out,
                fields, ysend, zsend, ylo, yhi, zlo, zhi,
                scat, r1, piece, r2, mine, full, rowmine, rr1, rowsum, rr2,
                load_sem, ssem, rsem, gsem):
    gx, gy, gz = (lax.axis_index(n) for n in ("gx", "gy", "gz"))
    me = gy * GZ + gz

    def plane_id(k):
        other = lax.rem(me + k, PLANE)
        return other, (gx, other // GZ, lax.rem(other, GZ))

    def line_id(k):
        return (lax.rem(gx + k, GX), gy, gz)

    load = pltpu.make_async_copy(flow, fields.at[0, :, pl.ds(1, 8)], load_sem)
    load.start()
    barrier = pltpu.get_barrier_semaphore()

    def greet_plane(k, carry):
        pl.semaphore_signal(barrier, inc=1, device_id=plane_id(k)[1], device_id_type=MESH)
        return carry

    def greet_line(k, carry):
        pl.semaphore_signal(barrier, inc=1, device_id=line_id(k), device_id_type=MESH)
        return carry

    lax.fori_loop(1, GX, greet_line, 0)
    lax.fori_loop(1, PLANE, greet_plane, 0)

    gram = jnp.zeros((128, 128), F32)
    for c in range(3):
        gram = gram + lax.dot_general(bt[c], bt[c], (((1,), (1,)), ((), ())), precision=HIGH,
                                      preferred_element_type=F32)
    for i in range(PLANE):
        scat[i] = gram[4 * i:4 * i + 4]

    load.wait()
    lane8 = iota((8, 128), 1)

    def first(x, faces):
        for c in range(4):
            faces = pack(fields[0, c, x + 1], c, x, faces, lane8, ysend.at[0])
        return faces

    zsend[0] = lax.fori_loop(0, 8, first, jnp.zeros((8, 128), F32))
    pl.semaphore_wait(barrier, GX - 1 + PLANE - 1)

    right = {
        "gx": (lax.rem(gx + 1, GX), gy, gz), "gy": (gx, lax.rem(gy + 1, GY), gz),
        "gz": (gx, gy, lax.rem(gz + 1, GZ)),
    }
    left = {
        "gx": (lax.rem(gx + GX - 1, GX), gy, gz), "gy": (gx, lax.rem(gy + GY - 1, GY), gz),
        "gz": (gx, gy, lax.rem(gz + GZ - 1, GZ)),
    }

    def exchange(s):
        f = fields.at[s]
        moves = [
            (f.at[:, pl.ds(1, 1)], f.at[:, pl.ds(9, 1)], left["gx"]),
            (f.at[:, pl.ds(8, 1)], f.at[:, pl.ds(0, 1)], right["gx"]),
            (ysend.at[s, 0], yhi.at[s], left["gy"]),
            (ysend.at[s, 1], ylo.at[s], right["gy"]),
            (zsend.at[s], zhi.at[s], left["gz"]),
            (zsend.at[s], zlo.at[s], right["gz"]),
        ]
        copies = [
            pltpu.make_async_remote_copy(src_ref=a, dst_ref=b, send_sem=ssem.at[s, i],
                                         recv_sem=rsem.at[s, i], device_id=d, device_id_type=MESH)
            for i, (a, b, d) in enumerate(moves)
        ]
        for copy in copies:
            copy.start()
        return copies

    def scatter(k, carry):
        other, where = plane_id(k)
        pltpu.make_async_remote_copy(src_ref=scat.at[other], dst_ref=r1.at[me], send_sem=gsem.at[0],
                                     recv_sem=gsem.at[1], device_id=where, device_id_type=MESH).start()
        return carry

    def spread(src, dst, sems, line):
        def go(k, carry):
            where = line_id(k) if line else plane_id(k)[1]
            pltpu.make_async_remote_copy(src_ref=src, dst_ref=dst.at[gx if line else me],
                                         send_sem=gsem.at[sems], recv_sem=gsem.at[sems + 1],
                                         device_id=where, device_id_type=MESH).start()
            return carry
        lax.fori_loop(1, GX if line else PLANE, go, 0)

    def settle(buf, sem, count):
        part = buf.at[pl.ds(0, count)]
        pltpu.make_async_copy(part, part, gsem.at[sem]).wait()

    def step(s, dst, weights):
        ynext = ysend.at[s + 1] if s < 2 else None
        faces = stencil(fields.at[s], fields.at[0], dst, ylo.at[s], yhi.at[s], zlo.at[s],
                        zhi.at[s], ynext, gy, weights)
        if s < 2:
            zsend[s + 1] = faces

    copies = exchange(0)
    everything = list(copies)
    lax.fori_loop(1, PLANE, scatter, 0)
    r1[me] = scat[me]
    for c in copies:
        c.wait_recv()
    step(0, fields.at[1], None)
    copies = exchange(1)
    everything += copies

    settle(r1, 1, PLANE - 1)
    total = r1[0]
    for i in range(1, PLANE):
        total = total + r1[i]
    piece[...] = total
    spread(piece, r2, 2, True)
    r2[gx] = total

    for c in copies:
        c.wait_recv()
    step(1, fields.at[2], (0.75, 0.25))
    copies = exchange(2)
    everything += copies
    for c in copies:
        c.wait_recv()
    step(2, out, (1.0 / 3.0, 2.0 / 3.0))

    s = sample[...]
    rows = (iota((128, 256), 0) == s // 128).astype(F32)
    cols = iota((128, 256), 0) == lax.rem(s, 128)
    line = jnp.zeros((1, 128), F32)
    own = jnp.zeros((1, 1), F32)
    for c in range(3):
        velocity = out[c].reshape(128, 128)
        picked = lax.dot_general(velocity, rows, (((0,), (0,)), ((), ())), precision=HIGH,
                                 preferred_element_type=F32)
        snap = jnp.sum(jnp.where(cols, picked, 0.0), axis=0, keepdims=True)
        snap_out[c:c + 1] = snap
        both = lax.dot_general(jnp.broadcast_to(snap, (8, 256)), bt[c], (((1,), (1,)), ((), ())),
                               precision=HIGH, preferred_element_type=F32)
        line = line + both[0:1]
        own = own + jnp.sum(snap * snap, axis=1, keepdims=True)
    line = jnp.where(iota((1, 128), 1) == 127, own, line)
    rowmine[...] = line
    spread(rowmine, rr1, 6, False)
    rr1[me] = line

    settle(r2, 3, GX - 1)
    total = r2[0]
    for i in range(1, GX):
        total = total + r2[i]
    mine[...] = total
    spread(mine, full, 4, False)
    full[me] = total

    settle(rr1, 7, PLANE - 1)
    total = rr1[0]
    for i in range(1, PLANE):
        total = total + rr1[i]
    rowsum[...] = total
    spread(rowsum, rr2, 8, True)
    rr2[gx] = total

    settle(full, 5, PLANE - 1)
    for i in range(PLANE):
        gram_out[4 * i:4 * i + 4] = full[i]
    settle(rr2, 9, GX - 1)
    total = rr2[0]
    for i in range(1, GX):
        total = total + rr2[i]
    row_out[...] = total

    for c in everything:
        c.wait_send()
    settle(r1, 0, PLANE - 1)
    settle(r2, 2, GX - 1)
    settle(full, 4, PLANE - 1)
    settle(rr1, 6, PLANE - 1)
    settle(rr2, 8, GX - 1)


def factorize(a):
    w = (iota((128, 128), 0) == iota((128, 128), 1)).astype(F32)
    both = jnp.concatenate([a, w], axis=1)
    sub = iota((8, 256), 0)
    sub1 = iota((8, 1), 0)
    lane = iota((8, 128), 1)
    ups, invs = [], []
    for b in range(16):
        p = both[8 * b:8 * b + 8]
        diag = jnp.ones((8, 1), F32)
        for j in range(8):
            k = 8 * b + j
            col = p[:, k:k + 1]
            d = col[j:j + 1]
            diag = jnp.where(sub1 == j, d, diag)
            if j < 7:
                pivot = p[j:j + 1] * (1.0 / d)
                p = p - jnp.where(sub > j, col * pivot, 0.0)
        p = p * lax.rsqrt(diag)
        up = jnp.where(lane >= 8 * b + iota((8, 128), 0), p[:, :128], 0.0)
        inv = p[:, 128:]
        ups.append(up)
        invs.append(inv)
        if b < 15:
            both = both - lax.dot_general(up, jnp.concatenate([up, inv], axis=1),
                                          (((0,), (0,)), ((), ())), precision=HIGH,
                                          preferred_element_type=F32)
    return jnp.concatenate(ups, axis=0), jnp.concatenate(invs, axis=0)


def solve_kernel(bt, snap, gram, row, out, factor):
    r = row[...]
    low = jnp.where(iota((128, 128), 0) == 127, r, gram[...])
    full = jnp.where((iota((128, 128), 1) == 127) & (iota((128, 128), 0) < 127), low.T, low)
    upper, inverse = factorize(full * (1.0 / COUNT))
    factor[...] = upper
    last = iota((128, 256), 0) == 127
    for c in range(3):
        stacked = jnp.where(last, snap[c:c + 1], bt[c])
        out[c] = jnp.dot(inverse, stacked, precision=HIGH, preferred_element_type=F32)


def local(flow, basis, sample):
    bt = jnp.pad(jnp.transpose(basis, (1, 0, 2)), ((0, 0), (0, 1), (0, 0)))
    vm = pl.BlockSpec(memory_space=pltpu.VMEM)
    flow_next, snap, gram, row = pl.pallas_call(
        comm_kernel,
        out_shape=[
            jax.ShapeDtypeStruct((4, 8, 16, 128), F32),
            jax.ShapeDtypeStruct((3, 256), F32),
            jax.ShapeDtypeStruct((128, 128), F32),
            jax.ShapeDtypeStruct((1, 128), F32),
        ],
        in_specs=[pl.BlockSpec(memory_space=pl.ANY), vm, vm],
        out_specs=[vm] * 4,
        scratch_shapes=[
            pltpu.VMEM((3, 4, 10, 16, 128), F32),
            pltpu.VMEM((3, 2, 4, 8, 128), F32),
            pltpu.VMEM((3, 8, 128), F32),
            pltpu.VMEM((3, 4, 8, 128), F32),
            pltpu.VMEM((3, 4, 8, 128), F32),
            pltpu.VMEM((3, 8, 128), F32),
            pltpu.VMEM((3, 8, 128), F32),
            pltpu.VMEM((PLANE, 4, 128), F32),
            pltpu.VMEM((PLANE, 4, 128), F32),
            pltpu.VMEM((4, 128), F32),
            pltpu.VMEM((GX, 4, 128), F32),
            pltpu.VMEM((4, 128), F32),
            pltpu.VMEM((PLANE, 4, 128), F32),
            pltpu.VMEM((1, 128), F32),
            pltpu.VMEM((PLANE, 1, 128), F32),
            pltpu.VMEM((1, 128), F32),
            pltpu.VMEM((GX, 1, 128), F32),
            pltpu.SemaphoreType.DMA,
            pltpu.SemaphoreType.DMA((3, 6)),
            pltpu.SemaphoreType.DMA((3, 6)),
            pltpu.SemaphoreType.DMA((10,)),
        ],
        compiler_params=pltpu.CompilerParams(collective_id=0, has_side_effects=True),
    )(flow, bt, sample.reshape(1, 256))
    out, factor = pl.pallas_call(
        solve_kernel,
        out_shape=[
            jax.ShapeDtypeStruct((3, 128, 256), F32),
            jax.ShapeDtypeStruct((128, 128), F32),
        ],
        in_specs=[vm] * 4,
        out_specs=[vm] * 2,
    )(bt, snap, gram, row)
    return (flow_next, jnp.transpose(out, (1, 0, 2)), factor)


def solution(mesh):
    return jax.shard_map(
        local,
        mesh=mesh,
        in_specs=(
            P(None, "gx", "gy", "gz"),
            P(None, None, ("gx", "gy", "gz")),
            P(("gx", "gy", "gz")),
        ),
        out_specs=(P(None, "gx", "gy", "gz"), P(None, None, ("gx", "gy", "gz")), P()),
        check_vma=False,
    )
```

time: 583 us -> 70.8 us (0.12)
  waiting for transfers between devices: 467 us -> 0 us
  Pallas kernels: 0 us -> 67.5 us
  starting transfers between devices: 52 us -> 0 us
  other arithmetic: 33.4 us -> 0 us
  between operations: 14.5 us -> 0.65 us
  local copies, waits for them, and re-layouts: 12.7 us -> 2.49 us
    psum x1 -> x0, waiting for transfers between devices: 433 us -> none  [local(): gram = lax.psum(local_gram, ('gx', 'gy', 'gz')) / count]
    pallas_call x0 -> x2, Pallas kernels: none -> 67.5 us  [the longest x1 49.2 us: local(): pl.pallas_call(comm_kernel, out_shape=[jax.ShapeDtypeStruct((4, 8, 16, 12...]
    ppermute x18 -> x0, starting transfers between devices: 52 us -> none  [the longest x9 32.1 us: padded(): lax.ppermute(lax.slice_in_dim(block, 0, width, axis=dim), axis, backward)]
    ppermute x18 -> x0, waiting for transfers between devices: 34.3 us -> none  [the longest x9 25.5 us: padded(): lax.ppermute(lax.slice_in_dim(block, 0, width, axis=dim), axis, backward)]
    another operation x4 -> x0, other arithmetic: 22.2 us -> none  [the longest x3 12.4 us: local(): lower = jnp.linalg.cholesky(gram)]
    slice x8 -> x0, local copies, waits for them, and re-layouts: 6.39 us -> none  [the longest x2 4.74 us: local(): velocity = flow_next[:3].reshape(3, -1)]
  transfers between devices with their start and end apart: 19 -> 0, of which waited for: 11 -> 0; matrix products, arithmetic and copies ran while one was open for 1% -> 0% of each run, Pallas kernels for 0% -> 0%
where the time goes in v1:
time: 70.8 us; the launch traced here: 70.6 us
  Pallas kernels  67.5 us (95%)
  local copies, waits for them, and re-layouts  2.49 us (4%)
    pallas_call x1, Pallas kernels, local(): pl.pallas_call(comm_kernel, out_shape=[jax.ShapeDtypeStruct((4, 8, 16, 12...  49.2 us
    pallas_call x1, Pallas kernels, local(): pl.pallas_call(solve_kernel, out_shape=[jax.ShapeDtypeStruct((3, 128, 256...  18.3 us
    pad x1, local copies, waits for them, and re-layouts, local(): bt = jnp.pad(jnp.transpose(basis, (1, 0, 2)), ((0, 0), (0, 1), (0, 0)))  1.79 us

profile of v1, /device:TPU:1, one launch (start us, length us, event | category | flops | bytes accessed | tf_op | source)
XLA Modules:
  0.0 70.6 jit_solution(4782305052944655107)
XLA Ops:
  0.6 1.8 %pad.4.bt = f32[3,128,256]{2,1,0:T(8,128)} pad(f32[3,127,256]{2,1,0:T(8,128)} %bitcast.3, f32[]{:T(128)} %constant.2.clone.1), padding=0_0x0_1x0_0 | pad | bytes 783364 | tf_op jit(solution)/shard_map/jit(_pad)/pad | solution.py:310
  2.4 49.2 %shard_map.58 = (f32[4,8,16,128]{3,2,1,0:T(8,128)}, f32[3,256]{1,0:T(4,128)}, f32[128,128]{1,0:T(8,128)}, f32[1,128]{1,0:T(1,128)}) custom-call(f32[4,8,16,128]{3,2,1,0:T(8,128)} %flow.1, f32[3,128,256]{2,1,0:T(8,128)} %pad.4.bt, s32[1,256]{1,0:T(1,128)} %bitcast.4), custom_call_target="tpu_custom_call" | custom-call | tf_op jit(solution)/shard_map/pallas_call | solution.py:312
  51.6 0.0 copy-start
  51.6 18.3 %shard_map.59 = (f32[3,128,256]{2,1,0:T(8,128)}, f32[128,128]{1,0:T(8,128)}) custom-call(f32[3,128,256]{2,1,0:T(8,128)} %pad.4.bt, f32[3,256]{1,0:T(4,128)} %get-tuple-element.10.snap, f32[128,128]{1,0:T(8,128)} %get-tuple-element.11.gram, f32[1,128]{1,0:T(1,128)} %get-tuple-element.12.row), custom_call_target="tpu_custom_call" | custom-call | tf_op jit(solution)/shard_map/pallas_call | solution.py:347
  69.9 0.0 copy-done
  69.9 0.7 copy.7
Async XLA Ops:
  51.6 18.3 %copy-start = (f32[4,8,16,128]{3,2,1,0:T(8,128)S(1)}, f32[4,8,16,128]{3,2,1,0:T(8,128)}, u32[]{:S(2)}) copy-start(f32[4,8,16,128]{3,2,1,0:T(8,128)} %get-tuple-element.18) | copy-start | bytes 786436

commit v2 on v1

--- a/solution.py
+++ b/solution.py
@@ -1,3 +1,5 @@
+import functools
+
 import jax
 import jax.numpy as jnp
 from jax import lax
@@ -11,6 +13,7 @@
 DRIVING = 0.5
 GX, GY, GZ = 16, 4, 8
 PLANE = GY * GZ
+FIRST = 6
 COUNT = 3.0 * 256 * GX * GY * GZ
 MESH = pl.DeviceIdType.MESH
 HIGH = lax.Precision.HIGHEST
@@ -82,8 +85,8 @@
     return faces
 
 
-def comm_kernel(flow, bt, sample, out, snap_out, gram_out, row_out,
-                fields, ysend, zsend, ylo, yhi, zlo, zhi,
+def comm_kernel(flow, basis, sample, out, snap_out, upper, inverse, row_out,
+                bt, both, fields, ysend, zsend, ylo, yhi, zlo, zhi,
                 scat, r1, piece, r2, mine, full, rowmine, rr1, rowsum, rr2,
                 load_sem, ssem, rsem, gsem):
     gx, gy, gz = (lax.axis_index(n) for n in ("gx", "gy", "gz"))
@@ -96,7 +99,9 @@
     def line_id(k):
         return (lax.rem(gx + k, GX), gy, gz)
 
-    load = pltpu.make_async_copy(flow, fields.at[0, :, pl.ds(1, 8)], load_sem)
+    load = pltpu.make_async_copy(flow, fields.at[0, :, pl.ds(1, 8)], load_sem.at[0])
+    load_bt = pltpu.make_async_copy(basis, bt, load_sem.at[1])
+    load_bt.start()
     load.start()
     barrier = pltpu.get_barrier_semaphore()
 
@@ -111,10 +116,12 @@
     lax.fori_loop(1, GX, greet_line, 0)
     lax.fori_loop(1, PLANE, greet_plane, 0)
 
+    load_bt.wait()
     gram = jnp.zeros((128, 128), F32)
+    blank = jnp.zeros((1, 256), F32)
     for c in range(3):
-        gram = gram + lax.dot_general(bt[c], bt[c], (((1,), (1,)), ((), ())), precision=HIGH,
-                                      preferred_element_type=F32)
+        block = jnp.concatenate([bt[c], blank], axis=0)
+        gram = gram + times_transposed(block, block)
     for i in range(PLANE):
         scat[i] = gram[4 * i:4 * i + 4]
 
@@ -208,28 +215,6 @@
     everything += copies
     for c in copies:
         c.wait_recv()
-    step(2, out, (1.0 / 3.0, 2.0 / 3.0))
-
-    s = sample[...]
-    rows = (iota((128, 256), 0) == s // 128).astype(F32)
-    cols = iota((128, 256), 0) == lax.rem(s, 128)
-    line = jnp.zeros((1, 128), F32)
-    own = jnp.zeros((1, 1), F32)
-    for c in range(3):
-        velocity = out[c].reshape(128, 128)
-        picked = lax.dot_general(velocity, rows, (((0,), (0,)), ((), ())), precision=HIGH,
-                                 preferred_element_type=F32)
-        snap = jnp.sum(jnp.where(cols, picked, 0.0), axis=0, keepdims=True)
-        snap_out[c:c + 1] = snap
-        both = lax.dot_general(jnp.broadcast_to(snap, (8, 256)), bt[c], (((1,), (1,)), ((), ())),
-                               precision=HIGH, preferred_element_type=F32)
-        line = line + both[0:1]
-        own = own + jnp.sum(snap * snap, axis=1, keepdims=True)
-    line = jnp.where(iota((1, 128), 1) == 127, own, line)
-    rowmine[...] = line
-    spread(rowmine, rr1, 6, False)
-    rr1[me] = line
-
     settle(r2, 3, GX - 1)
     total = r2[0]
     for i in range(1, GX):
@@ -237,6 +222,33 @@
     mine[...] = total
     spread(mine, full, 4, False)
     full[me] = total
+    step(2, out, (1.0 / 3.0, 2.0 / 3.0))
+
+    s = sample[...]
+    rows = (iota((128, 256), 0) == s // 128).astype(F32)
+    cols = iota((128, 256), 0) == lax.rem(s, 128)
+    line = jnp.zeros((1, 128), F32)
+    for c in range(3):
+        velocity = out[c].reshape(128, 128)
+        picked = lax.dot_general(velocity, rows, (((0,), (0,)), ((), ())), precision=HIGH,
+                                 preferred_element_type=F32)
+        snap = jnp.sum(jnp.where(cols, picked, 0.0), axis=0, keepdims=True)
+        snap_out[c:c + 1] = snap
+        block = jnp.concatenate([bt[c], snap], axis=0)
+        line = line + times_transposed(jnp.broadcast_to(snap, (8, 256)), block)[0:1]
+    rowmine[...] = line
+    spread(rowmine, rr1, 6, False)
+    rr1[me] = line
+
+    settle(full, 5, PLANE - 1)
+    unit = iota((4, 128), 1)
+    for i in range(PLANE):
+        below = 4 * i + iota((4, 128), 0)
+        corner = (below == 127) & (unit == 127)
+        both[4 * i:4 * i + 4, :128] = jnp.where(corner, 1.0, full[i] * (1.0 / COUNT))
+        both[4 * i:4 * i + 4, 128:] = (unit == below).astype(F32)
+    panel = functools.partial(eliminate, both=both, upper=upper, inverse=inverse)
+    lax.fori_loop(0, FIRST, panel, 0)
 
     settle(rr1, 7, PLANE - 1)
     total = rr1[0]
@@ -245,10 +257,7 @@
     rowsum[...] = total
     spread(rowsum, rr2, 8, True)
     rr2[gx] = total
-
-    settle(full, 5, PLANE - 1)
-    for i in range(PLANE):
-        gram_out[4 * i:4 * i + 4] = full[i]
+    lax.fori_loop(FIRST, 16, panel, 0)
     settle(rr2, 9, GX - 1)
     total = rr2[0]
     for i in range(1, GX):
@@ -264,62 +273,87 @@
     settle(rr2, 8, GX - 1)
 
 
-def factorize(a):
-    w = (iota((128, 128), 0) == iota((128, 128), 1)).astype(F32)
-    both = jnp.concatenate([a, w], axis=1)
-    sub = iota((8, 256), 0)
-    sub1 = iota((8, 1), 0)
+def eliminate(b, carry, both, upper, inverse):
+    rows = pl.ds(pl.multiple_of(8 * b, 8), 8)
+    p = both[rows, :]
+    left, right = p[:, :128], p[:, 128:]
+    near = pltpu.roll(left, lax.rem(128 - 8 * b, 128), 1)
+    full = (8, 128)
+    e = [[None] * 8 for _ in range(8)]
+    for k in range(8):
+        col = jnp.broadcast_to(near[:, k:k + 1], full)
+        for i in range(k, 8):
+            e[i][k] = jnp.broadcast_to(col[i:i + 1], full)
+    xs = [jnp.broadcast_to(left[i:i + 1], full) for i in range(8)]
+    ys = [jnp.broadcast_to(right[i:i + 1], full) for i in range(8)]
+    sub = iota(full, 0)
+    up, inv = xs[0], ys[0]
+    for k in range(8):
+        scale = lax.rsqrt(e[k][k])
+        up = jnp.where(sub == k, xs[k] * scale, up)
+        inv = jnp.where(sub == k, ys[k] * scale, inv)
+        if k < 7:
+            recip = 1.0 / e[k][k]
+            for i in range(k + 1, 8):
+                part = e[i][k] * recip
+                for m in range(k + 1, i + 1):
+                    e[i][m] = e[i][m] - part * e[m][k]
+                xs[i] = xs[i] - part * xs[k]
+                ys[i] = ys[i] - part * ys[k]
+    up = jnp.where(iota(full, 1) >= 8 * b + sub, up, 0.0)
+    upper[rows, :] = up
+    inverse[rows, :] = inv
+    both[...] = both[...] - lax.dot_general(
+        up, jnp.concatenate([up, inv], axis=1), (((0,), (0,)), ((), ())), precision=HIGH,
+        preferred_element_type=F32)
+    return carry
+
+
+def times_transposed(a, b):
+    return lax.dot_general(a, b, (((1,), (1,)), ((), ())), precision=HIGH,
+                           preferred_element_type=F32)
+
+
+def solve_kernel(bt, snap, upper, inverse, row, flow, out, factor, flow_out):
+    flow_out[...] = flow[...]
     lane = iota((8, 128), 1)
-    ups, invs = [], []
-    for b in range(16):
-        p = both[8 * b:8 * b + 8]
-        diag = jnp.ones((8, 1), F32)
-        for j in range(8):
-            k = 8 * b + j
-            col = p[:, k:k + 1]
-            d = col[j:j + 1]
-            diag = jnp.where(sub1 == j, d, diag)
-            if j < 7:
-                pivot = p[j:j + 1] * (1.0 / d)
-                p = p - jnp.where(sub > j, col * pivot, 0.0)
-        p = p * lax.rsqrt(diag)
-        up = jnp.where(lane >= 8 * b + iota((8, 128), 0), p[:, :128], 0.0)
-        inv = p[:, 128:]
-        ups.append(up)
-        invs.append(inv)
-        if b < 15:
-            both = both - lax.dot_general(up, jnp.concatenate([up, inv], axis=1),
-                                          (((0,), (0,)), ((), ())), precision=HIGH,
-                                          preferred_element_type=F32)
-    return jnp.concatenate(ups, axis=0), jnp.concatenate(invs, axis=0)
-
-
-def solve_kernel(bt, snap, gram, row, out, factor):
-    r = row[...]
-    low = jnp.where(iota((128, 128), 0) == 127, r, gram[...])
-    full = jnp.where((iota((128, 128), 1) == 127) & (iota((128, 128), 0) < 127), low.T, low)
-    upper, inverse = factorize(full * (1.0 / COUNT))
-    factor[...] = upper
-    last = iota((128, 256), 0) == 127
+    w = inverse[...]
+    r = jnp.broadcast_to(row[...] * (1.0 / COUNT), (8, 128))
+    inner = jnp.where(lane < 127, r, 0.0)
+    y = jnp.where(lane < 127, times_transposed(inner, w), 0.0)
+    corner = jnp.sum(r - inner, axis=1, keepdims=True) - jnp.sum(y * y, axis=1, keepdims=True)
+    scale = lax.rsqrt(corner)
+    last = -jnp.dot(y, w, precision=HIGH, preferred_element_type=F32)
+    last = jnp.where(lane == 127, 1.0, last) * scale
+    w = jnp.where(iota((128, 128), 0) == 127, last[0:1], w)
+    edge = jnp.where(lane == 127, corner * scale, y)
+    square = jnp.where(iota((128, 128), 1) == 127, jnp.broadcast_to(edge[0:1], (128, 128)).T, upper[...])
+    factor[...] = square
     for c in range(3):
-        stacked = jnp.where(last, snap[c:c + 1], bt[c])
-        out[c] = jnp.dot(inverse, stacked, precision=HIGH, preferred_element_type=F32)
+        stacked = jnp.concatenate([bt[c], snap[c:c + 1]], axis=0)
+        out[c] = jnp.dot(w, stacked, precision=HIGH, preferred_element_type=F32)
 
 
 def local(flow, basis, sample):
-    bt = jnp.pad(jnp.transpose(basis, (1, 0, 2)), ((0, 0), (0, 1), (0, 0)))
+    bt = jnp.transpose(basis, (1, 0, 2))
     vm = pl.BlockSpec(memory_space=pltpu.VMEM)
-    flow_next, snap, gram, row = pl.pallas_call(
+    hbm = pl.BlockSpec(memory_space=pltpu.HBM)
+    square = jax.ShapeDtypeStruct((128, 128), F32)
+    whole = jax.ShapeDtypeStruct((4, 8, 16, 128), F32)
+    flow_next, snap, upper, inverse, row = pl.pallas_call(
         comm_kernel,
         out_shape=[
-            jax.ShapeDtypeStruct((4, 8, 16, 128), F32),
+            whole,
             jax.ShapeDtypeStruct((3, 256), F32),
-            jax.ShapeDtypeStruct((128, 128), F32),
+            square,
+            square,
             jax.ShapeDtypeStruct((1, 128), F32),
         ],
-        in_specs=[pl.BlockSpec(memory_space=pl.ANY), vm, vm],
-        out_specs=[vm] * 4,
+        in_specs=[hbm, hbm, vm],
+        out_specs=[vm] * 5,
         scratch_shapes=[
+            pltpu.VMEM((3, 127, 256), F32),
+            pltpu.VMEM((128, 256), F32),
             pltpu.VMEM((3, 4, 10, 16, 128), F32),
             pltpu.VMEM((3, 2, 4, 8, 128), F32),
             pltpu.VMEM((3, 8, 128), F32),
@@ -337,22 +371,21 @@
             pltpu.VMEM((PLANE, 1, 128), F32),
             pltpu.VMEM((1, 128), F32),
             pltpu.VMEM((GX, 1, 128), F32),
-            pltpu.SemaphoreType.DMA,
+            pltpu.SemaphoreType.DMA((2,)),
             pltpu.SemaphoreType.DMA((3, 6)),
             pltpu.SemaphoreType.DMA((3, 6)),
             pltpu.SemaphoreType.DMA((10,)),
         ],
-        compiler_params=pltpu.CompilerParams(collective_id=0, has_side_effects=True),
+        compiler_params=pltpu.CompilerParams(collective_id=0, has_side_effects=True,
+                                             vmem_limit_bytes=16 << 20),
     )(flow, bt, sample.reshape(1, 256))
-    out, factor = pl.pallas_call(
+    out, factor, flow_next = pl.pallas_call(
         solve_kernel,
-        out_shape=[
-            jax.ShapeDtypeStruct((3, 128, 256), F32),
-            jax.ShapeDtypeStruct((128, 128), F32),
-        ],
-        in_specs=[vm] * 4,
-        out_specs=[vm] * 2,
-    )(bt, snap, gram, row)
+        out_shape=[jax.ShapeDtypeStruct((3, 128, 256), F32), square, whole],
+        in_specs=[vm] * 6,
+        out_specs=[vm] * 3,
+        compiler_params=pltpu.CompilerParams(vmem_limit_bytes=16 << 20),
+    )(bt, snap, upper, inverse, row, flow_next)
     return (flow_next, jnp.transpose(out, (1, 0, 2)), factor)
 
 

time: 70.8 us -> 53.8 us (0.76)
  Pallas kernels: 67.5 us -> 50.3 us
    pallas_call x1, Pallas kernels: 18.3 us -> 1.74 us  [local(): pl.pallas_call(solve_kernel, out_shape=[jax.ShapeDtypeStruct((3, 128, 256...]
    unnamed x3 -> x8, local copies, waits for them, and re-layouts: 0.71 us -> 2.62 us
    pad x1 -> x0, local copies, waits for them, and re-layouts: 1.79 us -> none  [local(): bt = jnp.pad(jnp.transpose(basis, (1, 0, 2)), ((0, 0), (0, 1), (0, 0)))]
where the time goes in v2:
time: 53.8 us; the launch traced here: 53.6 us
  Pallas kernels  50.3 us (93%)
  local copies, waits for them, and re-layouts  2.62 us (5%)
  between operations  0.66 us (1%)
    pallas_call x1, Pallas kernels, local(): pl.pallas_call(comm_kernel, out_shape=[whole, jax.ShapeDtypeStruct((3, 25...  48.6 us
    unnamed x8, local copies, waits for them, and re-layouts  2.62 us
    pallas_call x1, Pallas kernels, local(): pl.pallas_call(solve_kernel, out_shape=[jax.ShapeDtypeStruct((3, 128, 256...  1.74 us

profile of v2, /device:TPU:1, one launch (start us, length us, event | category | flops | bytes accessed | tf_op | source)
XLA Modules:
  0.0 53.6 jit_solution(16077351538966291591)
XLA Ops:
  0.6 0.0 copy-start.3
  0.6 0.7 %copy-done.3 = s32[256]{0:T(256)S(1)} copy-done((s32[256]{0:T(256)S(1)}, s32[256]{0:T(256)}, u32[]{:S(2)}) %copy-start.3) | copy-done | bytes 1048
  1.3 0.0 copy-start
  1.3 1.0 %copy-done = f32[127,3,256]{2,0,1:T(8,128)S(1)} copy-done((f32[127,3,256]{2,0,1:T(8,128)S(1)}, f32[127,3,256]{2,0,1:T(8,128)}, u32[]{:S(2)}) %copy-start) | copy-done | bytes 390168
  2.3 0.0 copy-start.2
  2.3 0.9 %copy-done.2 = f32[4,8,16,128]{3,2,1,0:T(8,128)S(1)} copy-done((f32[4,8,16,128]{3,2,1,0:T(8,128)S(1)}, f32[4,8,16,128]{3,2,1,0:T(8,128)}, u32[]{:S(2)}) %copy-start.2) | copy-done | bytes 262168
  3.3 0.0 copy-start.1
  3.3 48.6 %shard_map.58 = (f32[4,8,16,128]{3,2,1,0:T(8,128)S(1)}, f32[3,256]{1,0:T(4,128)S(1)}, f32[128,128]{1,0:T(8,128)S(1)}, f32[128,128]{1,0:T(8,128)S(1)}, f32[1,128]{1,0:T(1,128)S(1)}) custom-call(f32[4,8,16,128]{3,2,1,0:T(8,128)S(1)} %copy-done.2, f32[3,127,256]{2,1,0:T(8,128)S(1)} %bitcast.3, s32[1,256]{1,0:T(1,128)S(1)} %bitcast.5), custom_call_target="tpu_custom_call" | custom-call | tf_op jit(solution)/shard_map/pallas_call | solution.py:343
  51.8 0.0 copy-done.1
  51.8 1.7 %shard_map.59 = (f32[3,128,256]{2,1,0:T(8,128)}, f32[128,128]{1,0:T(8,128)}, f32[4,8,16,128]{3,2,1,0:T(8,128)}) custom-call(f32[3,127,256]{2,1,0:T(8,128)S(1)} %bitcast.4, f32[3,256]{1,0:T(4,128)S(1)} %get-tuple-element.11.snap, f32[128,128]{1,0:T(8,128)S(1)} %get-tuple-element.12.upper, f32[128,128]{1,0:T(8,128)S(1)} %get-tuple-element.13.inverse, ...), custom_call_target="tpu_custom_call" | custom-call | tf_op jit(solution)/shard_map/pallas_call | solution.py:382
Async XLA Ops:
  0.6 0.7 %copy-start.3 = (s32[256]{0:T(256)S(1)}, s32[256]{0:T(256)}, u32[]{:S(2)}) copy-start(s32[256]{0:T(256)} %param.5) | copy-start | bytes 3076
  1.3 1.0 %copy-start = (f32[127,3,256]{2,0,1:T(8,128)S(1)}, f32[127,3,256]{2,0,1:T(8,128)}, u32[]{:S(2)}) copy-start(f32[127,3,256]{2,0,1:T(8,128)} %param.4) | copy-start | bytes 1170436
  2.3 0.9 %copy-start.2 = (f32[4,8,16,128]{3,2,1,0:T(8,128)S(1)}, f32[4,8,16,128]{3,2,1,0:T(8,128)}, u32[]{:S(2)}) copy-start(f32[4,8,16,128]{3,2,1,0:T(8,128)} %flow.1) | copy-start | bytes 786436
  3.3 48.6 %copy-start.1 = (f32[127,3,256]{2,0,1:T(8,128)S(1)}, f32[127,3,256]{2,0,1:T(8,128)}, u32[]{:S(2)}) copy-start(f32[127,3,256]{2,0,1:T(8,128)} %param.4) | copy-start | bytes 1170436

commit v3 on v2

--- a/solution.py
+++ b/solution.py
@@ -13,7 +13,7 @@
 DRIVING = 0.5
 GX, GY, GZ = 16, 4, 8
 PLANE = GY * GZ
-FIRST = 6
+UNROLL = 4
 COUNT = 3.0 * 256 * GX * GY * GZ
 MESH = pl.DeviceIdType.MESH
 HIGH = lax.Precision.HIGHEST
@@ -30,7 +30,7 @@
     row = iota((16, 128), 0)
     low_z, high_z = zlo[...], zhi[...]
 
-    def body(x, faces):
+    def plane(x, faces):
         zl = pltpu.roll(low_z, 64 - 8 * x, 1)
         zh = pltpu.roll(high_z, lax.rem(128 - 8 * x, 128), 1)
         mid = [field[c, x + 1] for c in range(4)]
@@ -71,7 +71,12 @@
                 faces = pack(new, c, x, faces, lane8, ynext)
         return faces
 
-    return lax.fori_loop(0, 8, body, jnp.zeros((8, 128), F32))
+    def body(i, faces):
+        for d in range(UNROLL):
+            faces = plane(UNROLL * i + d, faces)
+        return faces
+
+    return lax.fori_loop(0, 8 // UNROLL, body, jnp.zeros((8, 128), F32))
 
 
 def pack(new, c, x, faces, lane8, ynext):
@@ -85,10 +90,10 @@
     return faces
 
 
-def comm_kernel(flow, basis, sample, out, snap_out, upper, inverse, row_out,
-                bt, both, fields, ysend, zsend, ylo, yhi, zlo, zhi,
+def comm_kernel(flow, basis, sample, out, snap_out, upper_out, inverse_out, row_out,
+                bt, both, upper, inverse, snaps, row, fields, ysend, zsend, ylo, yhi, zlo, zhi,
                 scat, r1, piece, r2, mine, full, rowmine, rr1, rowsum, rr2,
-                load_sem, ssem, rsem, gsem):
+                load_sem, store_sem, ssem, rsem, gsem, know):
     gx, gy, gz = (lax.axis_index(n) for n in ("gx", "gy", "gz"))
     me = gy * GZ + gz
 
@@ -96,64 +101,49 @@
         other = lax.rem(me + k, PLANE)
         return other, (gx, other // GZ, lax.rem(other, GZ))
 
-    def line_id(k):
-        return (lax.rem(gx + k, GX), gy, gz)
-
+    def at(dx=0, dy=0, dz=0):
+        return (lax.rem(gx + dx + GX, GX), lax.rem(gy + dy + GY, GY), lax.rem(gz + dz + GZ, GZ))
+
+    def tell(sem, where):
+        pl.semaphore_signal(sem, inc=1, device_id=where, device_id_type=MESH)
+
+    barrier = pltpu.get_barrier_semaphore()
+    for d in (1, -1):
+        tell(barrier, at(dx=d))
+    for d in range(1, GY):
+        tell(barrier, at(dy=d))
+    for d in range(1, GZ):
+        tell(barrier, at(dz=d))
     load = pltpu.make_async_copy(flow, fields.at[0, :, pl.ds(1, 8)], load_sem.at[0])
+    load.start()
     load_bt = pltpu.make_async_copy(basis, bt, load_sem.at[1])
     load_bt.start()
-    load.start()
-    barrier = pltpu.get_barrier_semaphore()
-
-    def greet_plane(k, carry):
-        pl.semaphore_signal(barrier, inc=1, device_id=plane_id(k)[1], device_id_type=MESH)
-        return carry
-
-    def greet_line(k, carry):
-        pl.semaphore_signal(barrier, inc=1, device_id=line_id(k), device_id_type=MESH)
-        return carry
-
-    lax.fori_loop(1, GX, greet_line, 0)
-    lax.fori_loop(1, PLANE, greet_plane, 0)
-
-    load_bt.wait()
-    gram = jnp.zeros((128, 128), F32)
-    blank = jnp.zeros((1, 256), F32)
-    for c in range(3):
-        block = jnp.concatenate([bt[c], blank], axis=0)
-        gram = gram + times_transposed(block, block)
-    for i in range(PLANE):
-        scat[i] = gram[4 * i:4 * i + 4]
-
     load.wait()
     lane8 = iota((8, 128), 1)
 
-    def first(x, faces):
-        for c in range(4):
-            faces = pack(fields[0, c, x + 1], c, x, faces, lane8, ysend.at[0])
+    def first(i, faces):
+        for d in range(UNROLL):
+            x = UNROLL * i + d
+            for c in range(4):
+                faces = pack(fields[0, c, x + 1], c, x, faces, lane8, ysend.at[0])
         return faces
 
-    zsend[0] = lax.fori_loop(0, 8, first, jnp.zeros((8, 128), F32))
-    pl.semaphore_wait(barrier, GX - 1 + PLANE - 1)
-
-    right = {
-        "gx": (lax.rem(gx + 1, GX), gy, gz), "gy": (gx, lax.rem(gy + 1, GY), gz),
-        "gz": (gx, gy, lax.rem(gz + 1, GZ)),
-    }
-    left = {
-        "gx": (lax.rem(gx + GX - 1, GX), gy, gz), "gy": (gx, lax.rem(gy + GY - 1, GY), gz),
-        "gz": (gx, gy, lax.rem(gz + GZ - 1, GZ)),
-    }
+    zsend[0] = lax.fori_loop(0, 8 // UNROLL, first, jnp.zeros((8, 128), F32))
+    pl.semaphore_wait(barrier, 2 + GY - 1 + GZ - 1)
+    for d in range(1, GZ):
+        tell(know.at[0], at(dz=d))
+    for d in (1, -1):
+        tell(know.at[1], at(dx=d))
 
     def exchange(s):
         f = fields.at[s]
         moves = [
-            (f.at[:, pl.ds(1, 1)], f.at[:, pl.ds(9, 1)], left["gx"]),
-            (f.at[:, pl.ds(8, 1)], f.at[:, pl.ds(0, 1)], right["gx"]),
-            (ysend.at[s, 0], yhi.at[s], left["gy"]),
-            (ysend.at[s, 1], ylo.at[s], right["gy"]),
-            (zsend.at[s], zhi.at[s], left["gz"]),
-            (zsend.at[s], zlo.at[s], right["gz"]),
+            (f.at[:, pl.ds(1, 1)], f.at[:, pl.ds(9, 1)], at(dx=-1)),
+            (f.at[:, pl.ds(8, 1)], f.at[:, pl.ds(0, 1)], at(dx=1)),
+            (ysend.at[s, 0], yhi.at[s], at(dy=-1)),
+            (ysend.at[s, 1], ylo.at[s], at(dy=1)),
+            (zsend.at[s], zhi.at[s], at(dz=-1)),
+            (zsend.at[s], zlo.at[s], at(dz=1)),
         ]
         copies = [
             pltpu.make_async_remote_copy(src_ref=a, dst_ref=b, send_sem=ssem.at[s, i],
@@ -172,7 +162,7 @@
 
     def spread(src, dst, sems, line):
         def go(k, carry):
-            where = line_id(k) if line else plane_id(k)[1]
+            where = at(dx=k) if line else plane_id(k)[1]
             pltpu.make_async_remote_copy(src_ref=src, dst_ref=dst.at[gx if line else me],
                                          send_sem=gsem.at[sems], recv_sem=gsem.at[sems + 1],
                                          device_id=where, device_id_type=MESH).start()
@@ -182,6 +172,12 @@
     def settle(buf, sem, count):
         part = buf.at[pl.ds(0, count)]
         pltpu.make_async_copy(part, part, gsem.at[sem]).wait()
+
+    def add_up(buf, count):
+        parts = [buf[i] for i in range(count)]
+        while len(parts) > 1:
+            parts = [a + b for a, b in zip(parts[::2], parts[1::2])]
+        return parts[0]
 
     def step(s, dst, weights):
         ynext = ysend.at[s + 1] if s < 2 else None
@@ -192,53 +188,77 @@
 
     copies = exchange(0)
     everything = list(copies)
+
+    load_bt.wait()
+    gram = jnp.zeros((128, 128), F32)
+    blank = jnp.zeros((1, 256), F32)
+    for c in range(3):
+        block = jnp.concatenate([bt[c], blank], axis=0)
+        gram = gram + times_transposed(block, block)
+    for i in range(PLANE):
+        scat[i] = gram[4 * i:4 * i + 4]
+    pl.semaphore_wait(know.at[0], GZ - 1)
     lax.fori_loop(1, PLANE, scatter, 0)
     r1[me] = scat[me]
+    pl.semaphore_wait(know.at[1], 2)
+    for d in (2, -2):
+        tell(know.at[2], at(dx=d))
+
     for c in copies:
         c.wait_recv()
     step(0, fields.at[1], None)
     copies = exchange(1)
     everything += copies
 
+    pl.semaphore_wait(know.at[2], 2)
+    for d in (4, -4):
+        tell(know.at[3], at(dx=d))
+    for c in copies:
+        c.wait_recv()
     settle(r1, 1, PLANE - 1)
-    total = r1[0]
-    for i in range(1, PLANE):
-        total = total + r1[i]
+    pl.semaphore_wait(know.at[3], 2)
+    total = add_up(r1, PLANE)
     piece[...] = total
     spread(piece, r2, 2, True)
     r2[gx] = total
 
-    for c in copies:
-        c.wait_recv()
     step(1, fields.at[2], (0.75, 0.25))
     copies = exchange(2)
     everything += copies
     for c in copies:
         c.wait_recv()
-    settle(r2, 3, GX - 1)
-    total = r2[0]
-    for i in range(1, GX):
-        total = total + r2[i]
-    mine[...] = total
-    spread(mine, full, 4, False)
-    full[me] = total
-    step(2, out, (1.0 / 3.0, 2.0 / 3.0))
+    result = fields.at[3]
+    step(2, result, (1.0 / 3.0, 2.0 / 3.0))
+    stores = [pltpu.make_async_copy(result.at[:, pl.ds(0, 8)], out, store_sem.at[0])]
+    stores[0].start()
 
     s = sample[...]
     rows = (iota((128, 256), 0) == s // 128).astype(F32)
     cols = iota((128, 256), 0) == lax.rem(s, 128)
     line = jnp.zeros((1, 128), F32)
     for c in range(3):
-        velocity = out[c].reshape(128, 128)
+        velocity = fields[3, c, 0:8].reshape(128, 128)
         picked = lax.dot_general(velocity, rows, (((0,), (0,)), ((), ())), precision=HIGH,
                                  preferred_element_type=F32)
         snap = jnp.sum(jnp.where(cols, picked, 0.0), axis=0, keepdims=True)
-        snap_out[c:c + 1] = snap
+        snaps[c:c + 1] = snap
         block = jnp.concatenate([bt[c], snap], axis=0)
         line = line + times_transposed(jnp.broadcast_to(snap, (8, 256)), block)[0:1]
     rowmine[...] = line
     spread(rowmine, rr1, 6, False)
     rr1[me] = line
+
+    settle(r2, 3, GX - 1)
+    total = add_up(r2, GX)
+    mine[...] = total
+    spread(mine, full, 4, False)
+    full[me] = total
+
+    settle(rr1, 7, PLANE - 1)
+    total = add_up(rr1, PLANE)
+    rowsum[...] = total
+    spread(rowsum, rr2, 8, True)
+    rr2[gx] = total
 
     settle(full, 5, PLANE - 1)
     unit = iota((4, 128), 1)
@@ -248,21 +268,15 @@
         both[4 * i:4 * i + 4, :128] = jnp.where(corner, 1.0, full[i] * (1.0 / COUNT))
         both[4 * i:4 * i + 4, 128:] = (unit == below).astype(F32)
     panel = functools.partial(eliminate, both=both, upper=upper, inverse=inverse)
-    lax.fori_loop(0, FIRST, panel, 0)
-
-    settle(rr1, 7, PLANE - 1)
-    total = rr1[0]
-    for i in range(1, PLANE):
-        total = total + rr1[i]
-    rowsum[...] = total
-    spread(rowsum, rr2, 8, True)
-    rr2[gx] = total
-    lax.fori_loop(FIRST, 16, panel, 0)
+    lax.fori_loop(0, 16, panel, 0)
+    for src, dst in ((snaps, snap_out), (upper, upper_out), (inverse, inverse_out)):
+        stores.append(pltpu.make_async_copy(src, dst, store_sem.at[len(stores)]))
+        stores[-1].start()
+
     settle(rr2, 9, GX - 1)
-    total = rr2[0]
-    for i in range(1, GX):
-        total = total + rr2[i]
-    row_out[...] = total
+    row[...] = add_up(rr2, GX)
+    stores.append(pltpu.make_async_copy(row, row_out, store_sem.at[4]))
+    stores[-1].start()
 
     for c in everything:
         c.wait_send()
@@ -271,6 +285,8 @@
     settle(full, 4, PLANE - 1)
     settle(rr1, 6, PLANE - 1)
     settle(rr2, 8, GX - 1)
+    for c in stores:
+        c.wait()
 
 
 def eliminate(b, carry, both, upper, inverse):
@@ -314,8 +330,15 @@
                            preferred_element_type=F32)
 
 
-def solve_kernel(bt, snap, upper, inverse, row, flow, out, factor, flow_out):
-    flow_out[...] = flow[...]
+def solve_kernel(bt_in, snap_in, upper_in, inverse_in, row_in, flow_in, out_to, factor_to, flow_to,
+                 bt, snap, upper, inverse, row, flow, out, factor, sems):
+    pairs = ((row_in, row), (inverse_in, inverse), (upper_in, upper), (snap_in, snap),
+             (bt_in, bt), (flow_in, flow))
+    loads = [pltpu.make_async_copy(a, b, sems.at[i]) for i, (a, b) in enumerate(pairs)]
+    for copy in loads:
+        copy.start()
+    for copy in loads[:4]:
+        copy.wait()
     lane = iota((8, 128), 1)
     w = inverse[...]
     r = jnp.broadcast_to(row[...] * (1.0 / COUNT), (8, 128))
@@ -329,9 +352,22 @@
     edge = jnp.where(lane == 127, corner * scale, y)
     square = jnp.where(iota((128, 128), 1) == 127, jnp.broadcast_to(edge[0:1], (128, 128)).T, upper[...])
     factor[...] = square
+    stores = []
+
+    def store(a, b):
+        stores.append(pltpu.make_async_copy(a, b, sems.at[6 + len(stores)]))
+        stores[-1].start()
+
+    store(factor, factor_to)
+    for copy in loads[4:]:
+        copy.wait()
+    store(flow, flow_to)
     for c in range(3):
         stacked = jnp.concatenate([bt[c], snap[c:c + 1]], axis=0)
         out[c] = jnp.dot(w, stacked, precision=HIGH, preferred_element_type=F32)
+        store(out.at[c], out_to.at[c])
+    for copy in stores:
+        copy.wait()
 
 
 def local(flow, basis, sample):
@@ -350,11 +386,15 @@
             jax.ShapeDtypeStruct((1, 128), F32),
         ],
         in_specs=[hbm, hbm, vm],
-        out_specs=[vm] * 5,
+        out_specs=[hbm] * 5,
         scratch_shapes=[
             pltpu.VMEM((3, 127, 256), F32),
             pltpu.VMEM((128, 256), F32),
-            pltpu.VMEM((3, 4, 10, 16, 128), F32),
+            pltpu.VMEM((128, 128), F32),
+            pltpu.VMEM((128, 128), F32),
+            pltpu.VMEM((3, 256), F32),
+            pltpu.VMEM((1, 128), F32),
+            pltpu.VMEM((4, 4, 10, 16, 128), F32),
             pltpu.VMEM((3, 2, 4, 8, 128), F32),
             pltpu.VMEM((3, 8, 128), F32),
             pltpu.VMEM((3, 4, 8, 128), F32),
@@ -372,19 +412,30 @@
             pltpu.VMEM((1, 128), F32),
             pltpu.VMEM((GX, 1, 128), F32),
             pltpu.SemaphoreType.DMA((2,)),
+            pltpu.SemaphoreType.DMA((5,)),
             pltpu.SemaphoreType.DMA((3, 6)),
             pltpu.SemaphoreType.DMA((3, 6)),
             pltpu.SemaphoreType.DMA((10,)),
+            pltpu.SemaphoreType.REGULAR((4,)),
         ],
-        compiler_params=pltpu.CompilerParams(collective_id=0, has_side_effects=True,
-                                             vmem_limit_bytes=16 << 20),
+        compiler_params=pltpu.CompilerParams(collective_id=0, has_side_effects=True),
     )(flow, bt, sample.reshape(1, 256))
     out, factor, flow_next = pl.pallas_call(
         solve_kernel,
         out_shape=[jax.ShapeDtypeStruct((3, 128, 256), F32), square, whole],
-        in_specs=[vm] * 6,
-        out_specs=[vm] * 3,
-        compiler_params=pltpu.CompilerParams(vmem_limit_bytes=16 << 20),
+        in_specs=[hbm] * 6,
+        out_specs=[hbm] * 3,
+        scratch_shapes=[
+            pltpu.VMEM((3, 127, 256), F32),
+            pltpu.VMEM((3, 256), F32),
+            pltpu.VMEM((128, 128), F32),
+            pltpu.VMEM((128, 128), F32),
+            pltpu.VMEM((1, 128), F32),
+            pltpu.VMEM((4, 8, 16, 128), F32),
+            pltpu.VMEM((3, 128, 256), F32),
+            pltpu.VMEM((128, 128), F32),
+            pltpu.SemaphoreType.DMA((11,)),
+        ],
     )(bt, snap, upper, inverse, row, flow_next)
     return (flow_next, jnp.transpose(out, (1, 0, 2)), factor)
 

time: 53.8 us -> 48.6 us (0.903)
  local copies, waits for them, and re-layouts: 2.62 us -> 0 us
  Pallas kernels: 50.3 us -> 47.8 us
    pallas_call x1, Pallas kernels: 48.6 us -> 45.1 us  [local(): pl.pallas_call(comm_kernel, out_shape=[whole, jax.ShapeDtypeStruct((3, 25...]
    unnamed x8 -> x0, local copies, waits for them, and re-layouts: 2.62 us -> none
    pallas_call x1, Pallas kernels: 1.74 us -> 2.67 us  [local(): pl.pallas_call(solve_kernel, out_shape=[jax.ShapeDtypeStruct((3, 128, 256...]
where the time goes in v3:
time: 48.6 us; the launch traced here: 48.4 us
  Pallas kernels  47.8 us (98%)
  between operations  0.64 us (1%)
    pallas_call x1, Pallas kernels, local(): pl.pallas_call(comm_kernel, out_shape=[whole, jax.ShapeDtypeStruct((3, 25...  45.1 us
    pallas_call x1, Pallas kernels, local(): pl.pallas_call(solve_kernel, out_shape=[jax.ShapeDtypeStruct((3, 128, 256...  2.67 us

profile of v3, /device:TPU:1, one launch (start us, length us, event | category | flops | bytes accessed | tf_op | source)
XLA Modules:
  0.0 48.4 jit_solution(11062995775662923483)
XLA Ops:
  0.6 45.1 %shard_map.58 = (f32[4,8,16,128]{3,2,1,0:T(8,128)}, f32[3,256]{1,0:T(4,128)}, f32[128,128]{1,0:T(8,128)}, f32[128,128]{1,0:T(8,128)}, f32[1,128]{1,0:T(1,128)}) custom-call(f32[4,8,16,128]{3,2,1,0:T(8,128)} %flow.1, f32[3,127,256]{2,1,0:T(8,128)} %bitcast.3, s32[1,256]{1,0:T(1,128)} %bitcast.5), custom_call_target="tpu_custom_call" | custom-call | tf_op jit(solution)/shard_map/pallas_call | solution.py:379
  45.7 2.7 %shard_map.59 = (f32[3,128,256]{2,1,0:T(8,128)}, f32[128,128]{1,0:T(8,128)}, f32[4,8,16,128]{3,2,1,0:T(8,128)}) custom-call(f32[3,127,256]{2,1,0:T(8,128)} %bitcast.4, f32[3,256]{1,0:T(4,128)} %get-tuple-element.11.snap_in, f32[128,128]{1,0:T(8,128)} %get-tuple-element.12.upper_in, f32[128,128]{1,0:T(8,128)} %get-tuple-element.13.inverse_in, ...), custom_call_target="tpu_custom_call" | custom-call | tf_op jit(solution)/shard_map/pallas_call | solution.py:423

commit v4 on v3

--- a/solution.py
+++ b/solution.py
@@ -268,7 +268,7 @@
         both[4 * i:4 * i + 4, :128] = jnp.where(corner, 1.0, full[i] * (1.0 / COUNT))
         both[4 * i:4 * i + 4, 128:] = (unit == below).astype(F32)
     panel = functools.partial(eliminate, both=both, upper=upper, inverse=inverse)
-    lax.fori_loop(0, 16, panel, 0)
+    lax.fori_loop(0, 8, panel, 0)
     for src, dst in ((snaps, snap_out), (upper, upper_out), (inverse, inverse_out)):
         stores.append(pltpu.make_async_copy(src, dst, store_sem.at[len(stores)]))
         stores[-1].start()
@@ -289,39 +289,62 @@
         c.wait()
 
 
-def eliminate(b, carry, both, upper, inverse):
-    rows = pl.ds(pl.multiple_of(8 * b, 8), 8)
-    p = both[rows, :]
-    left, right = p[:, :128], p[:, 128:]
-    near = pltpu.roll(left, lax.rem(128 - 8 * b, 128), 1)
+def pivots(near, start, left, right, later=None):
     full = (8, 128)
     e = [[None] * 8 for _ in range(8)]
     for k in range(8):
-        col = jnp.broadcast_to(near[:, k:k + 1], full)
+        col = jnp.broadcast_to(near[:, start + k:start + k + 1], full)
         for i in range(k, 8):
             e[i][k] = jnp.broadcast_to(col[i:i + 1], full)
-    xs = [jnp.broadcast_to(left[i:i + 1], full) for i in range(8)]
-    ys = [jnp.broadcast_to(right[i:i + 1], full) for i in range(8)]
+    parts = [left, right]
+    if later is not None:
+        below = [jnp.broadcast_to(later[0][:, start + k:start + k + 1], full) for k in range(8)]
+        parts.append(near)
+        lows = [later[1], later[2], later[0]]
+    rows = [[jnp.broadcast_to(a[i:i + 1], full) for i in range(8)] for a in parts]
     sub = iota(full, 0)
-    up, inv = xs[0], ys[0]
+    up, inv = rows[0][0], rows[1][0]
     for k in range(8):
         scale = lax.rsqrt(e[k][k])
-        up = jnp.where(sub == k, xs[k] * scale, up)
-        inv = jnp.where(sub == k, ys[k] * scale, inv)
-        if k < 7:
+        up = jnp.where(sub == k, rows[0][k] * scale, up)
+        inv = jnp.where(sub == k, rows[1][k] * scale, inv)
+        if k < 7 or later is not None:
             recip = 1.0 / e[k][k]
-            for i in range(k + 1, 8):
-                part = e[i][k] * recip
-                for m in range(k + 1, i + 1):
-                    e[i][m] = e[i][m] - part * e[m][k]
-                xs[i] = xs[i] - part * xs[k]
-                ys[i] = ys[i] - part * ys[k]
-    up = jnp.where(iota(full, 1) >= 8 * b + sub, up, 0.0)
+        for i in range(k + 1, 8):
+            part = e[i][k] * recip
+            for m in range(k + 1, i + 1):
+                e[i][m] = e[i][m] - part * e[m][k]
+            for x in rows:
+                x[i] = x[i] - part * x[k]
+        if later is not None:
+            part = below[k] * recip
+            for m in range(k + 1, 8):
+                below[m] = below[m] - part * e[m][k]
+            lows = [low - part * x[k] for low, x in zip(lows, rows)]
+    return (up, inv, lows) if later is not None else (up, inv)
+
+
+def eliminate(b, carry, both, upper, inverse):
+    rows = pl.ds(pl.multiple_of(16 * b, 16), 16) if not isinstance(b, int) else pl.ds(16 * b, 16)
+    p = both[rows, :]
+    left, right = p[:, :128], p[:, 128:]
+    near, start = left, 0
+    if isinstance(b, int):
+        start = 16 * b
+    else:
+        near = pltpu.roll(left, lax.rem(128 - 16 * b, 128), 1)
+    up_a, inv_a, (left_b, right_b, near_b) = pivots(
+        near[:8], start, left[:8], right[:8], (near[8:], left[8:], right[8:]))
+    up_b, inv_b = pivots(near_b, start + 8, left_b, right_b)
+    up = jnp.concatenate([up_a, up_b], axis=0)
+    inv = jnp.concatenate([inv_a, inv_b], axis=0)
+    up = jnp.where(iota((16, 128), 1) >= 16 * b + iota((16, 128), 0), up, 0.0)
     upper[rows, :] = up
     inverse[rows, :] = inv
-    both[...] = both[...] - lax.dot_general(
-        up, jnp.concatenate([up, inv], axis=1), (((0,), (0,)), ((), ())), precision=HIGH,
-        preferred_element_type=F32)
+    if not isinstance(b, int) or b < 7:
+        both[...] = both[...] - lax.dot_general(
+            up, jnp.concatenate([up, inv], axis=1), (((0,), (0,)), ((), ())), precision=HIGH,
+            preferred_element_type=F32)
     return carry
 
 

time: 48.6 us -> 45.8 us (0.942)
  Pallas kernels: 47.8 us -> 45 us
    pallas_call x1, Pallas kernels: 45.1 us -> 42.3 us  [local(): pl.pallas_call(comm_kernel, out_shape=[whole, jax.ShapeDtypeStruct((3, 25...]
where the time goes in v4:
time: 45.8 us; the launch traced here: 45.6 us
  Pallas kernels  45 us (98%)
  between operations  0.64 us (1%)
    pallas_call x1, Pallas kernels, local(): pl.pallas_call(comm_kernel, out_shape=[whole, jax.ShapeDtypeStruct((3, 25...  42.3 us
    pallas_call x1, Pallas kernels, local(): pl.pallas_call(solve_kernel, out_shape=[jax.ShapeDtypeStruct((3, 128, 256...  2.67 us

profile of v4, /device:TPU:1, one launch (start us, length us, event | category | flops | bytes accessed | tf_op | source)
XLA Modules:
  0.0 45.6 jit_solution(18249649826407836810)
XLA Ops:
  0.6 42.3 %shard_map.58 = (f32[4,8,16,128]{3,2,1,0:T(8,128)}, f32[3,256]{1,0:T(4,128)}, f32[128,128]{1,0:T(8,128)}, f32[128,128]{1,0:T(8,128)}, f32[1,128]{1,0:T(1,128)}) custom-call(f32[4,8,16,128]{3,2,1,0:T(8,128)} %flow.1, f32[3,127,256]{2,1,0:T(8,128)} %bitcast.3, s32[1,256]{1,0:T(1,128)} %bitcast.5), custom_call_target="tpu_custom_call" | custom-call | tf_op jit(solution)/shard_map/pallas_call | solution.py:402
  42.9 2.7 %shard_map.59 = (f32[3,128,256]{2,1,0:T(8,128)}, f32[128,128]{1,0:T(8,128)}, f32[4,8,16,128]{3,2,1,0:T(8,128)}) custom-call(f32[3,127,256]{2,1,0:T(8,128)} %bitcast.4, f32[3,256]{1,0:T(4,128)} %get-tuple-element.11.snap_in, f32[128,128]{1,0:T(8,128)} %get-tuple-element.12.upper_in, f32[128,128]{1,0:T(8,128)} %get-tuple-element.13.inverse_in, ...), custom_call_target="tpu_custom_call" | custom-call | tf_op jit(solution)/shard_map/pallas_call | solution.py:446

commit v5 on v4

--- a/solution.py
+++ b/solution.py
@@ -24,7 +24,7 @@
     return lax.broadcasted_iota(jnp.int32, shape, dim)
 
 
-def stencil(field, flow, out, ylo, yhi, zlo, zhi, ynext, gy, weights):
+def stencil(field, flow, out, ylo, yhi, zlo, zhi, ynext, gy, weights, early):
     lane = iota((16, 128), 1)
     lane8 = iota((8, 128), 1)
     row = iota((16, 128), 0)
@@ -32,7 +32,7 @@
 
     def plane(x, faces):
         zl = pltpu.roll(low_z, 64 - 8 * x, 1)
-        zh = pltpu.roll(high_z, lax.rem(128 - 8 * x, 128), 1)
+        zh = pltpu.roll(high_z, (128 - 8 * x) % 128, 1)
         mid = [field[c, x + 1] for c in range(4)]
         sx, sy, sz, lap = [], [], [], []
         for c in range(4):
@@ -72,11 +72,13 @@
         return faces
 
     def body(i, faces):
-        for d in range(UNROLL):
-            faces = plane(UNROLL * i + d, faces)
+        for x in (3 * i, 7 - 3 * i, 1 + 4 * i, 2 + 4 * i):
+            faces = plane(x, faces)
+        if early is not None:
+            pl.when(i == 0)(early)
         return faces
 
-    return lax.fori_loop(0, 8 // UNROLL, body, jnp.zeros((8, 128), F32))
+    return lax.fori_loop(0, 2, body, jnp.zeros((8, 128), F32))
 
 
 def pack(new, c, x, faces, lane8, ynext):
@@ -90,8 +92,8 @@
     return faces
 
 
-def comm_kernel(flow, basis, sample, out, snap_out, upper_out, inverse_out, row_out,
-                bt, both, upper, inverse, snaps, row, fields, ysend, zsend, ylo, yhi, zlo, zhi,
+def comm_kernel(flow, basis, sample_in, out, snap_out, upper_out, inverse_out, row_out,
+                sample, bt, both, upper, inverse, snaps, row, fields, ysend, zsend, ylo, yhi, zlo, zhi,
                 scat, r1, piece, r2, mine, full, rowmine, rr1, rowsum, rr2,
                 load_sem, store_sem, ssem, rsem, gsem, know):
     gx, gy, gz = (lax.axis_index(n) for n in ("gx", "gy", "gz"))
@@ -118,6 +120,8 @@
     load.start()
     load_bt = pltpu.make_async_copy(basis, bt, load_sem.at[1])
     load_bt.start()
+    load_sample = pltpu.make_async_copy(sample_in, sample, load_sem.at[2])
+    load_sample.start()
     load.wait()
     lane8 = iota((8, 128), 1)
 
@@ -135,9 +139,9 @@
     for d in (1, -1):
         tell(know.at[1], at(dx=d))
 
-    def exchange(s):
+    def moves(s, which=range(6)):
         f = fields.at[s]
-        moves = [
+        ends = [
             (f.at[:, pl.ds(1, 1)], f.at[:, pl.ds(9, 1)], at(dx=-1)),
             (f.at[:, pl.ds(8, 1)], f.at[:, pl.ds(0, 1)], at(dx=1)),
             (ysend.at[s, 0], yhi.at[s], at(dy=-1)),
@@ -145,14 +149,16 @@
             (zsend.at[s], zhi.at[s], at(dz=-1)),
             (zsend.at[s], zlo.at[s], at(dz=1)),
         ]
-        copies = [
-            pltpu.make_async_remote_copy(src_ref=a, dst_ref=b, send_sem=ssem.at[s, i],
-                                         recv_sem=rsem.at[s, i], device_id=d, device_id_type=MESH)
-            for i, (a, b, d) in enumerate(moves)
+        return [
+            pltpu.make_async_remote_copy(src_ref=ends[i][0], dst_ref=ends[i][1],
+                                         send_sem=ssem.at[s, i], recv_sem=rsem.at[s, i],
+                                         device_id=ends[i][2], device_id_type=MESH)
+            for i in which
         ]
-        for copy in copies:
+
+    def exchange(s, which):
+        for copy in moves(s, which):
             copy.start()
-        return copies
 
     def scatter(k, carry):
         other, where = plane_id(k)
@@ -181,13 +187,14 @@
 
     def step(s, dst, weights):
         ynext = ysend.at[s + 1] if s < 2 else None
+        early = functools.partial(exchange, s + 1, range(2)) if s < 2 else None
         faces = stencil(fields.at[s], fields.at[0], dst, ylo.at[s], yhi.at[s], zlo.at[s],
-                        zhi.at[s], ynext, gy, weights)
+                        zhi.at[s], ynext, gy, weights, early)
         if s < 2:
             zsend[s + 1] = faces
-
-    copies = exchange(0)
-    everything = list(copies)
+            exchange(s + 1, range(2, 6))
+
+    exchange(0, range(6))
 
     load_bt.wait()
     gram = jnp.zeros((128, 128), F32)
@@ -204,16 +211,14 @@
     for d in (2, -2):
         tell(know.at[2], at(dx=d))
 
-    for c in copies:
+    for c in moves(0):
         c.wait_recv()
     step(0, fields.at[1], None)
-    copies = exchange(1)
-    everything += copies
 
     pl.semaphore_wait(know.at[2], 2)
     for d in (4, -4):
         tell(know.at[3], at(dx=d))
-    for c in copies:
+    for c in moves(1):
         c.wait_recv()
     settle(r1, 1, PLANE - 1)
     pl.semaphore_wait(know.at[3], 2)
@@ -223,15 +228,14 @@
     r2[gx] = total
 
     step(1, fields.at[2], (0.75, 0.25))
-    copies = exchange(2)
-    everything += copies
-    for c in copies:
+    for c in moves(2):
         c.wait_recv()
     result = fields.at[3]
     step(2, result, (1.0 / 3.0, 2.0 / 3.0))
     stores = [pltpu.make_async_copy(result.at[:, pl.ds(0, 8)], out, store_sem.at[0])]
     stores[0].start()
 
+    load_sample.wait()
     s = sample[...]
     rows = (iota((128, 256), 0) == s // 128).astype(F32)
     cols = iota((128, 256), 0) == lax.rem(s, 128)
@@ -278,8 +282,9 @@
     stores.append(pltpu.make_async_copy(row, row_out, store_sem.at[4]))
     stores[-1].start()
 
-    for c in everything:
-        c.wait_send()
+    for s in range(3):
+        for c in moves(s):
+            c.wait_send()
     settle(r1, 0, PLANE - 1)
     settle(r2, 2, GX - 1)
     settle(full, 4, PLANE - 1)
@@ -395,7 +400,6 @@
 
 def local(flow, basis, sample):
     bt = jnp.transpose(basis, (1, 0, 2))
-    vm = pl.BlockSpec(memory_space=pltpu.VMEM)
     hbm = pl.BlockSpec(memory_space=pltpu.HBM)
     square = jax.ShapeDtypeStruct((128, 128), F32)
     whole = jax.ShapeDtypeStruct((4, 8, 16, 128), F32)
@@ -408,9 +412,10 @@
             square,
             jax.ShapeDtypeStruct((1, 128), F32),
         ],
-        in_specs=[hbm, hbm, vm],
+        in_specs=[hbm, hbm, hbm],
         out_specs=[hbm] * 5,
         scratch_shapes=[
+            pltpu.VMEM((1, 256), jnp.int32),
             pltpu.VMEM((3, 127, 256), F32),
             pltpu.VMEM((128, 256), F32),
             pltpu.VMEM((128, 128), F32),
@@ -434,14 +439,15 @@
             pltpu.VMEM((PLANE, 1, 128), F32),
             pltpu.VMEM((1, 128), F32),
             pltpu.VMEM((GX, 1, 128), F32),
-            pltpu.SemaphoreType.DMA((2,)),
+            pltpu.SemaphoreType.DMA((3,)),
             pltpu.SemaphoreType.DMA((5,)),
             pltpu.SemaphoreType.DMA((3, 6)),
             pltpu.SemaphoreType.DMA((3, 6)),
             pltpu.SemaphoreType.DMA((10,)),
             pltpu.SemaphoreType.REGULAR((4,)),
         ],
-        compiler_params=pltpu.CompilerParams(collective_id=0, has_side_effects=True),
+        compiler_params=pltpu.CompilerParams(collective_id=0, has_side_effects=True,
+                                             vmem_limit_bytes=56000000),
     )(flow, bt, sample.reshape(1, 256))
     out, factor, flow_next = pl.pallas_call(
         solve_kernel,
@@ -459,6 +465,7 @@
             pltpu.VMEM((128, 128), F32),
             pltpu.SemaphoreType.DMA((11,)),
         ],
+        compiler_params=pltpu.CompilerParams(vmem_limit_bytes=16 << 20),
     )(bt, snap, upper, inverse, row, flow_next)
     return (flow_next, jnp.transpose(out, (1, 0, 2)), factor)
 

time: 45.8 us -> 45.7 us (level)
  Pallas kernels: 45 us -> 44.1 us
  local copies, waits for them, and re-layouts: 0 us -> 0.73 us
    unnamed x0 -> x4, local copies, waits for them, and re-layouts: none -> 0.73 us
    pallas_call x1, Pallas kernels: 2.67 us -> 2.18 us  [local(): pl.pallas_call(solve_kernel, out_shape=[jax.ShapeDtypeStruct((3, 128, 256...]
where the time goes in v5:
time: 45.7 us; the launch traced here: 45.5 us
  Pallas kernels  44.1 us (96%)
  local copies, waits for them, and re-layouts  0.73 us (2%)
  between operations  0.66 us (1%)
    pallas_call x1, Pallas kernels, local(): pl.pallas_call(comm_kernel, out_shape=[whole, jax.ShapeDtypeStruct((3, 25...  42 us
    pallas_call x1, Pallas kernels, local(): pl.pallas_call(solve_kernel, out_shape=[jax.ShapeDtypeStruct((3, 128, 256...  2.18 us

profile of v5, /device:TPU:1, one launch (start us, length us, event | category | flops | bytes accessed | tf_op | source)
XLA Modules:
  0.0 45.5 jit_solution(11690144193035412938)
XLA Ops:
  0.6 0.0 copy-start
  0.6 0.0 copy-start.1
  0.7 0.7 %copy-done.1 = s32[256]{0:T(256)S(1)} copy-done((s32[256]{0:T(256)S(1)}, s32[256]{0:T(256)}, u32[]{:S(2)}) %copy-start.1) | copy-done | bytes 1048
  1.4 42.0 %shard_map.58 = (f32[4,8,16,128]{3,2,1,0:T(8,128)S(1)}, f32[3,256]{1,0:T(4,128)S(1)}, f32[128,128]{1,0:T(8,128)S(1)}, f32[128,128]{1,0:T(8,128)S(1)}, f32[1,128]{1,0:T(1,128)S(1)}) custom-call(f32[4,8,16,128]{3,2,1,0:T(8,128)} %flow.1, f32[3,127,256]{2,1,0:T(8,128)} %bitcast.3, s32[1,256]{1,0:T(1,128)S(1)} %bitcast.5), custom_call_target="tpu_custom_call" | custom-call | tf_op jit(solution)/shard_map/pallas_call | solution.py:406
  43.3 0.0 copy-done
  43.3 2.2 %shard_map.59 = (f32[3,128,256]{2,1,0:T(8,128)}, f32[128,128]{1,0:T(8,128)}, f32[4,8,16,128]{3,2,1,0:T(8,128)}) custom-call(f32[3,127,256]{2,1,0:T(8,128)S(1)} %bitcast.4, f32[3,256]{1,0:T(4,128)S(1)} %get-tuple-element.11.snap_in, f32[128,128]{1,0:T(8,128)S(1)} %get-tuple-element.12.upper_in, f32[128,128]{1,0:T(8,128)S(1)} %get-tuple-element.13.inverse_in, ...), custom_call_target="tpu_custom_call" | custom-call | tf_op jit(solution)/shard_map/pallas_call | solution.py:452
Async XLA Ops:
  0.6 42.7 %copy-start = (f32[127,3,256]{2,0,1:T(8,128)S(1)}, f32[127,3,256]{2,0,1:T(8,128)}, u32[]{:S(2)}) copy-start(f32[127,3,256]{2,0,1:T(8,128)} %param.4) | copy-start | bytes 1170436
  0.6 0.7 %copy-start.1 = (s32[256]{0:T(256)S(1)}, s32[256]{0:T(256)}, u32[]{:S(2)}) copy-start(s32[256]{0:T(256)} %param.5) | copy-start | bytes 3076

commit v6 on v5

--- a/solution.py
+++ b/solution.py
@@ -92,10 +92,10 @@
     return faces
 
 
-def comm_kernel(flow, basis, sample_in, out, snap_out, upper_out, inverse_out, row_out,
-                sample, bt, both, upper, inverse, snaps, row, fields, ysend, zsend, ylo, yhi, zlo, zhi,
+def comm_kernel(flow, basis, sample_in, result, snaps, upper, inverse, row,
+                sample, bt, both, fields, ysend, zsend, ylo, yhi, zlo, zhi,
                 scat, r1, piece, r2, mine, full, rowmine, rr1, rowsum, rr2,
-                load_sem, store_sem, ssem, rsem, gsem, know):
+                load_sem, ssem, rsem, gsem, know):
     gx, gy, gz = (lax.axis_index(n) for n in ("gx", "gy", "gz"))
     me = gy * GZ + gz
 
@@ -116,12 +116,20 @@
         tell(barrier, at(dy=d))
     for d in range(1, GZ):
         tell(barrier, at(dz=d))
+    load_bt = pltpu.make_async_copy(basis, bt, load_sem.at[1])
+    load_bt.start()
     load = pltpu.make_async_copy(flow, fields.at[0, :, pl.ds(1, 8)], load_sem.at[0])
     load.start()
-    load_bt = pltpu.make_async_copy(basis, bt, load_sem.at[1])
-    load_bt.start()
     load_sample = pltpu.make_async_copy(sample_in, sample, load_sem.at[2])
     load_sample.start()
+    load_bt.wait()
+    gram = jnp.zeros((128, 128), F32)
+    blank = jnp.zeros((1, 256), F32)
+    for c in range(3):
+        block = jnp.concatenate([bt[c], blank], axis=0)
+        gram = gram + times_transposed(block, block)
+    for i in range(PLANE):
+        scat[i] = gram[4 * i:4 * i + 4]
     load.wait()
     lane8 = iota((8, 128), 1)
 
@@ -196,14 +204,6 @@
 
     exchange(0, range(6))
 
-    load_bt.wait()
-    gram = jnp.zeros((128, 128), F32)
-    blank = jnp.zeros((1, 256), F32)
-    for c in range(3):
-        block = jnp.concatenate([bt[c], blank], axis=0)
-        gram = gram + times_transposed(block, block)
-    for i in range(PLANE):
-        scat[i] = gram[4 * i:4 * i + 4]
     pl.semaphore_wait(know.at[0], GZ - 1)
     lax.fori_loop(1, PLANE, scatter, 0)
     r1[me] = scat[me]
@@ -230,10 +230,7 @@
     step(1, fields.at[2], (0.75, 0.25))
     for c in moves(2):
         c.wait_recv()
-    result = fields.at[3]
     step(2, result, (1.0 / 3.0, 2.0 / 3.0))
-    stores = [pltpu.make_async_copy(result.at[:, pl.ds(0, 8)], out, store_sem.at[0])]
-    stores[0].start()
 
     load_sample.wait()
     s = sample[...]
@@ -241,7 +238,7 @@
     cols = iota((128, 256), 0) == lax.rem(s, 128)
     line = jnp.zeros((1, 128), F32)
     for c in range(3):
-        velocity = fields[3, c, 0:8].reshape(128, 128)
+        velocity = result[c].reshape(128, 128)
         picked = lax.dot_general(velocity, rows, (((0,), (0,)), ((), ())), precision=HIGH,
                                  preferred_element_type=F32)
         snap = jnp.sum(jnp.where(cols, picked, 0.0), axis=0, keepdims=True)
@@ -273,14 +270,8 @@
         both[4 * i:4 * i + 4, 128:] = (unit == below).astype(F32)
     panel = functools.partial(eliminate, both=both, upper=upper, inverse=inverse)
     lax.fori_loop(0, 8, panel, 0)
-    for src, dst in ((snaps, snap_out), (upper, upper_out), (inverse, inverse_out)):
-        stores.append(pltpu.make_async_copy(src, dst, store_sem.at[len(stores)]))
-        stores[-1].start()
-
     settle(rr2, 9, GX - 1)
     row[...] = add_up(rr2, GX)
-    stores.append(pltpu.make_async_copy(row, row_out, store_sem.at[4]))
-    stores[-1].start()
 
     for s in range(3):
         for c in moves(s):
@@ -290,8 +281,6 @@
     settle(full, 4, PLANE - 1)
     settle(rr1, 6, PLANE - 1)
     settle(rr2, 8, GX - 1)
-    for c in stores:
-        c.wait()
 
 
 def pivots(near, start, left, right, later=None):
@@ -358,17 +347,20 @@
                            preferred_element_type=F32)
 
 
-def solve_kernel(bt_in, snap_in, upper_in, inverse_in, row_in, flow_in, out_to, factor_to, flow_to,
-                 bt, snap, upper, inverse, row, flow, out, factor, sems):
-    pairs = ((row_in, row), (inverse_in, inverse), (upper_in, upper), (snap_in, snap),
-             (bt_in, bt), (flow_in, flow))
-    loads = [pltpu.make_async_copy(a, b, sems.at[i]) for i, (a, b) in enumerate(pairs)]
-    for copy in loads:
-        copy.start()
-    for copy in loads[:4]:
-        copy.wait()
+def solve_kernel(bt, snap, upper, inverse, row, flow, out_to, factor_to, flow_to,
+                 out, factor, sems):
+    stores = []
+
+    def store(a, b):
+        stores.append(pltpu.make_async_copy(a, b, sems.at[len(stores)]))
+        stores[-1].start()
+
+    store(flow, flow_to)
     lane = iota((8, 128), 1)
     w = inverse[...]
+    stacked = [jnp.concatenate([bt[c], snap[c:c + 1]], axis=0) for c in range(3)]
+    for c in range(3):
+        out[c] = jnp.dot(w, stacked[c], precision=HIGH, preferred_element_type=F32)
     r = jnp.broadcast_to(row[...] * (1.0 / COUNT), (8, 128))
     inner = jnp.where(lane < 127, r, 0.0)
     y = jnp.where(lane < 127, times_transposed(inner, w), 0.0)
@@ -376,23 +368,13 @@
     scale = lax.rsqrt(corner)
     last = -jnp.dot(y, w, precision=HIGH, preferred_element_type=F32)
     last = jnp.where(lane == 127, 1.0, last) * scale
-    w = jnp.where(iota((128, 128), 0) == 127, last[0:1], w)
     edge = jnp.where(lane == 127, corner * scale, y)
     square = jnp.where(iota((128, 128), 1) == 127, jnp.broadcast_to(edge[0:1], (128, 128)).T, upper[...])
     factor[...] = square
-    stores = []
-
-    def store(a, b):
-        stores.append(pltpu.make_async_copy(a, b, sems.at[6 + len(stores)]))
-        stores[-1].start()
-
     store(factor, factor_to)
-    for copy in loads[4:]:
-        copy.wait()
-    store(flow, flow_to)
     for c in range(3):
-        stacked = jnp.concatenate([bt[c], snap[c:c + 1]], axis=0)
-        out[c] = jnp.dot(w, stacked, precision=HIGH, preferred_element_type=F32)
+        out[c, 127:128] = jnp.dot(last, stacked[c], precision=HIGH,
+                                  preferred_element_type=F32)[0:1]
         store(out.at[c], out_to.at[c])
     for copy in stores:
         copy.wait()
@@ -400,6 +382,7 @@
 
 def local(flow, basis, sample):
     bt = jnp.transpose(basis, (1, 0, 2))
+    vm = pl.BlockSpec(memory_space=pltpu.VMEM)
     hbm = pl.BlockSpec(memory_space=pltpu.HBM)
     square = jax.ShapeDtypeStruct((128, 128), F32)
     whole = jax.ShapeDtypeStruct((4, 8, 16, 128), F32)
@@ -413,16 +396,12 @@
             jax.ShapeDtypeStruct((1, 128), F32),
         ],
         in_specs=[hbm, hbm, hbm],
-        out_specs=[hbm] * 5,
+        out_specs=[vm] * 5,
         scratch_shapes=[
             pltpu.VMEM((1, 256), jnp.int32),
             pltpu.VMEM((3, 127, 256), F32),
             pltpu.VMEM((128, 256), F32),
-            pltpu.VMEM((128, 128), F32),
-            pltpu.VMEM((128, 128), F32),
-            pltpu.VMEM((3, 256), F32),
-            pltpu.VMEM((1, 128), F32),
-            pltpu.VMEM((4, 4, 10, 16, 128), F32),
+            pltpu.VMEM((3, 4, 10, 16, 128), F32),
             pltpu.VMEM((3, 2, 4, 8, 128), F32),
             pltpu.VMEM((3, 8, 128), F32),
             pltpu.VMEM((3, 4, 8, 128), F32),
@@ -440,7 +419,6 @@
             pltpu.VMEM((1, 128), F32),
             pltpu.VMEM((GX, 1, 128), F32),
             pltpu.SemaphoreType.DMA((3,)),
-            pltpu.SemaphoreType.DMA((5,)),
             pltpu.SemaphoreType.DMA((3, 6)),
             pltpu.SemaphoreType.DMA((3, 6)),
             pltpu.SemaphoreType.DMA((10,)),
@@ -452,18 +430,12 @@
     out, factor, flow_next = pl.pallas_call(
         solve_kernel,
         out_shape=[jax.ShapeDtypeStruct((3, 128, 256), F32), square, whole],
-        in_specs=[hbm] * 6,
+        in_specs=[vm] * 6,
         out_specs=[hbm] * 3,
         scratch_shapes=[
-            pltpu.VMEM((3, 127, 256), F32),
-            pltpu.VMEM((3, 256), F32),
-            pltpu.VMEM((128, 128), F32),
-            pltpu.VMEM((128, 128), F32),
-            pltpu.VMEM((1, 128), F32),
-            pltpu.VMEM((4, 8, 16, 128), F32),
             pltpu.VMEM((3, 128, 256), F32),
             pltpu.VMEM((128, 128), F32),
-            pltpu.SemaphoreType.DMA((11,)),
+            pltpu.SemaphoreType.DMA((5,)),
         ],
         compiler_params=pltpu.CompilerParams(vmem_limit_bytes=16 << 20),
     )(bt, snap, upper, inverse, row, flow_next)

time: 45.7 us -> 44.8 us (0.980)
  Pallas kernels: 44.1 us -> 43.3 us
where the time goes in v6:
time: 44.8 us; the launch traced here: 44.7 us
  Pallas kernels  43.3 us (97%)
  local copies, waits for them, and re-layouts  0.73 us (2%)
  between operations  0.66 us (1%)
    pallas_call x1, Pallas kernels, local(): pl.pallas_call(comm_kernel, out_shape=[whole, jax.ShapeDtypeStruct((3, 25...  41.6 us
    pallas_call x1, Pallas kernels, local(): pl.pallas_call(solve_kernel, out_shape=[jax.ShapeDtypeStruct((3, 128, 256...  1.73 us

profile of v6, /device:TPU:1, one launch (start us, length us, event | category | flops | bytes accessed | tf_op | source)
XLA Modules:
  0.0 44.7 jit_solution(2315155384289111888)
XLA Ops:
  0.6 0.0 copy-start
  0.6 0.0 copy-start.1
  0.7 0.7 %copy-done.1 = s32[256]{0:T(256)S(1)} copy-done((s32[256]{0:T(256)S(1)}, s32[256]{0:T(256)}, u32[]{:S(2)}) %copy-start.1) | copy-done | bytes 1048
  1.4 41.6 %shard_map.58 = (f32[4,8,16,128]{3,2,1,0:T(8,128)S(1)}, f32[3,256]{1,0:T(4,128)S(1)}, f32[128,128]{1,0:T(8,128)S(1)}, f32[128,128]{1,0:T(8,128)S(1)}, f32[1,128]{1,0:T(1,128)S(1)}) custom-call(f32[4,8,16,128]{3,2,1,0:T(8,128)} %flow.1, f32[3,127,256]{2,1,0:T(8,128)} %bitcast.3, s32[1,256]{1,0:T(1,128)S(1)} %bitcast.5), custom_call_target="tpu_custom_call" | custom-call | tf_op jit(solution)/shard_map/pallas_call | solution.py:389
  42.9 0.0 copy-done
  43.0 1.7 %shard_map.59 = (f32[3,128,256]{2,1,0:T(8,128)}, f32[128,128]{1,0:T(8,128)}, f32[4,8,16,128]{3,2,1,0:T(8,128)}) custom-call(f32[3,127,256]{2,1,0:T(8,128)S(1)} %bitcast.4, f32[3,256]{1,0:T(4,128)S(1)} %get-tuple-element.11.snap, f32[128,128]{1,0:T(8,128)S(1)} %get-tuple-element.12.upper, f32[128,128]{1,0:T(8,128)S(1)} %get-tuple-element.13.inverse, ...), custom_call_target="tpu_custom_call" | custom-call | tf_op jit(solution)/shard_map/pallas_call | solution.py:430
Async XLA Ops:
  0.6 42.3 %copy-start = (f32[127,3,256]{2,0,1:T(8,128)S(1)}, f32[127,3,256]{2,0,1:T(8,128)}, u32[]{:S(2)}) copy-start(f32[127,3,256]{2,0,1:T(8,128)} %param.4) | copy-start | bytes 1170436
  0.6 0.7 %copy-start.1 = (s32[256]{0:T(256)S(1)}, s32[256]{0:T(256)}, u32[]{:S(2)}) copy-start(s32[256]{0:T(256)} %param.5) | copy-start | bytes 3076

commit v7 on v6

--- a/solution.py
+++ b/solution.py
@@ -204,22 +204,20 @@
 
     exchange(0, range(6))
 
+    pl.semaphore_wait(know.at[1], 2)
+    for d in (2, -2):
+        tell(know.at[2], at(dx=d))
     pl.semaphore_wait(know.at[0], GZ - 1)
     lax.fori_loop(1, PLANE, scatter, 0)
     r1[me] = scat[me]
-    pl.semaphore_wait(know.at[1], 2)
-    for d in (2, -2):
-        tell(know.at[2], at(dx=d))
 
     for c in moves(0):
         c.wait_recv()
-    step(0, fields.at[1], None)
-
     pl.semaphore_wait(know.at[2], 2)
     for d in (4, -4):
         tell(know.at[3], at(dx=d))
-    for c in moves(1):
-        c.wait_recv()
+    step(0, fields.at[1], None)
+
     settle(r1, 1, PLANE - 1)
     pl.semaphore_wait(know.at[3], 2)
     total = add_up(r1, PLANE)
@@ -227,6 +225,8 @@
     spread(piece, r2, 2, True)
     r2[gx] = total
 
+    for c in moves(1):
+        c.wait_recv()
     step(1, fields.at[2], (0.75, 0.25))
     for c in moves(2):
         c.wait_recv()

time: 44.8 us -> 44.1 us (0.984)
  Pallas kernels: 43.3 us -> 42.6 us
    pallas_call x1, Pallas kernels: 41.6 us -> 40.8 us  [local(): pl.pallas_call(comm_kernel, out_shape=[whole, jax.ShapeDtypeStruct((3, 25...]
where the time goes in v7:
time: 44.1 us; the launch traced here: 44 us
  Pallas kernels  42.6 us (97%)
  local copies, waits for them, and re-layouts  0.73 us (2%)
  between operations  0.66 us (1%)
    pallas_call x1, Pallas kernels, local(): pl.pallas_call(comm_kernel, out_shape=[whole, jax.ShapeDtypeStruct((3, 25...  40.8 us
    pallas_call x1, Pallas kernels, local(): pl.pallas_call(solve_kernel, out_shape=[jax.ShapeDtypeStruct((3, 128, 256...  1.73 us

profile of v7, /device:TPU:1, one launch (start us, length us, event | category | flops | bytes accessed | tf_op | source)
XLA Modules:
  0.0 44.0 jit_solution(11719313868479882154)
XLA Ops:
  0.6 0.0 copy-start
  0.6 0.0 copy-start.1
  0.7 0.7 %copy-done.1 = s32[256]{0:T(256)S(1)} copy-done((s32[256]{0:T(256)S(1)}, s32[256]{0:T(256)}, u32[]{:S(2)}) %copy-start.1) | copy-done | bytes 1048
  1.4 40.8 %shard_map.58 = (f32[4,8,16,128]{3,2,1,0:T(8,128)S(1)}, f32[3,256]{1,0:T(4,128)S(1)}, f32[128,128]{1,0:T(8,128)S(1)}, f32[128,128]{1,0:T(8,128)S(1)}, f32[1,128]{1,0:T(1,128)S(1)}) custom-call(f32[4,8,16,128]{3,2,1,0:T(8,128)} %flow.1, f32[3,127,256]{2,1,0:T(8,128)} %bitcast.3, s32[1,256]{1,0:T(1,128)S(1)} %bitcast.5), custom_call_target="tpu_custom_call" | custom-call | tf_op jit(solution)/shard_map/pallas_call | solution.py:389
  42.2 0.0 copy-done
  42.2 1.7 %shard_map.59 = (f32[3,128,256]{2,1,0:T(8,128)}, f32[128,128]{1,0:T(8,128)}, f32[4,8,16,128]{3,2,1,0:T(8,128)}) custom-call(f32[3,127,256]{2,1,0:T(8,128)S(1)} %bitcast.4, f32[3,256]{1,0:T(4,128)S(1)} %get-tuple-element.11.snap, f32[128,128]{1,0:T(8,128)S(1)} %get-tuple-element.12.upper, f32[128,128]{1,0:T(8,128)S(1)} %get-tuple-element.13.inverse, ...), custom_call_target="tpu_custom_call" | custom-call | tf_op jit(solution)/shard_map/pallas_call | solution.py:430
Async XLA Ops:
  0.6 41.6 %copy-start = (f32[127,3,256]{2,0,1:T(8,128)S(1)}, f32[127,3,256]{2,0,1:T(8,128)}, u32[]{:S(2)}) copy-start(f32[127,3,256]{2,0,1:T(8,128)} %param.4) | copy-start | bytes 1170436
  0.6 0.7 %copy-start.1 = (s32[256]{0:T(256)S(1)}, s32[256]{0:T(256)}, u32[]{:S(2)}) copy-start(s32[256]{0:T(256)} %param.5) | copy-start | bytes 3076

commit v8 on v7

--- a/solution.py
+++ b/solution.py
@@ -168,14 +168,18 @@
         for copy in moves(s, which):
             copy.start()
 
+    def far_first(k, count):
+        return 1 + lax.rem(k + count // 2 - 4, count - 1)
+
     def scatter(k, carry):
-        other, where = plane_id(k)
+        other, where = plane_id(far_first(k, PLANE))
         pltpu.make_async_remote_copy(src_ref=scat.at[other], dst_ref=r1.at[me], send_sem=gsem.at[0],
                                      recv_sem=gsem.at[1], device_id=where, device_id_type=MESH).start()
         return carry
 
     def spread(src, dst, sems, line):
         def go(k, carry):
+            k = far_first(k, GX if line else PLANE)
             where = at(dx=k) if line else plane_id(k)[1]
             pltpu.make_async_remote_copy(src_ref=src, dst_ref=dst.at[gx if line else me],
                                          send_sem=gsem.at[sems], recv_sem=gsem.at[sems + 1],

time: 44.1 us -> 44.8 us (1.016)
  Pallas kernels: 42.6 us -> 43.2 us
    pallas_call x1, Pallas kernels: 40.8 us -> 41.5 us  [local(): pl.pallas_call(comm_kernel, out_shape=[whole, jax.ShapeDtypeStruct((3, 25...]
where the time goes in v8:
time: 44.8 us; the launch traced here: 44.6 us
  Pallas kernels  43.2 us (96%)
  local copies, waits for them, and re-layouts  0.73 us (2%)
  between operations  0.66 us (1%)
    pallas_call x1, Pallas kernels, local(): pl.pallas_call(comm_kernel, out_shape=[whole, jax.ShapeDtypeStruct((3, 25...  41.5 us
    pallas_call x1, Pallas kernels, local(): pl.pallas_call(solve_kernel, out_shape=[jax.ShapeDtypeStruct((3, 128, 256...  1.73 us

profile of v8, /device:TPU:1, one launch (start us, length us, event | category | flops | bytes accessed | tf_op | source)
XLA Modules:
  0.0 44.6 jit_solution(17770871452286487607)
XLA Ops:
  0.6 0.0 copy-start
  0.6 0.0 copy-start.1
  0.7 0.7 %copy-done.1 = s32[256]{0:T(256)S(1)} copy-done((s32[256]{0:T(256)S(1)}, s32[256]{0:T(256)}, u32[]{:S(2)}) %copy-start.1) | copy-done | bytes 1048
  1.4 41.5 %shard_map.58 = (f32[4,8,16,128]{3,2,1,0:T(8,128)S(1)}, f32[3,256]{1,0:T(4,128)S(1)}, f32[128,128]{1,0:T(8,128)S(1)}, f32[128,128]{1,0:T(8,128)S(1)}, f32[1,128]{1,0:T(1,128)S(1)}) custom-call(f32[4,8,16,128]{3,2,1,0:T(8,128)} %flow.1, f32[3,127,256]{2,1,0:T(8,128)} %bitcast.3, s32[1,256]{1,0:T(1,128)S(1)} %bitcast.5), custom_call_target="tpu_custom_call" | custom-call | tf_op jit(solution)/shard_map/pallas_call | solution.py:393
  42.9 0.0 copy-done
  42.9 1.7 %shard_map.59 = (f32[3,128,256]{2,1,0:T(8,128)}, f32[128,128]{1,0:T(8,128)}, f32[4,8,16,128]{3,2,1,0:T(8,128)}) custom-call(f32[3,127,256]{2,1,0:T(8,128)S(1)} %bitcast.4, f32[3,256]{1,0:T(4,128)S(1)} %get-tuple-element.11.snap, f32[128,128]{1,0:T(8,128)S(1)} %get-tuple-element.12.upper, f32[128,128]{1,0:T(8,128)S(1)} %get-tuple-element.13.inverse, ...), custom_call_target="tpu_custom_call" | custom-call | tf_op jit(solution)/shard_map/pallas_call | solution.py:434
Async XLA Ops:
  0.6 42.3 %copy-start = (f32[127,3,256]{2,0,1:T(8,128)S(1)}, f32[127,3,256]{2,0,1:T(8,128)}, u32[]{:S(2)}) copy-start(f32[127,3,256]{2,0,1:T(8,128)} %param.4) | copy-start | bytes 1170436
  0.6 0.7 %copy-start.1 = (s32[256]{0:T(256)S(1)}, s32[256]{0:T(256)}, u32[]{:S(2)}) copy-start(s32[256]{0:T(256)} %param.5) | copy-start | bytes 3076
